TPU v7x, 128 devices: a whole 4x4x4 slice. The times are simulated.
128 devices in a mesh: sec: 4 (over x), dev: 32 (over y, z, core).
Axes of the slice: x: 4, y: 4, z: 4, core: 2. Of those that a mesh axis runs over, the one named last changes fastest.
Arguments:
- velocity: float32 [3, 64, 64, 4096], P(None, 'sec', None, 'dev'), may hold values from -6 to 6
- source: float32 [3, 64, 64, 4096], P(None, 'sec', None, 'dev'), may hold values from -6 to 6
- viscosity: float32 [64, 64, 4096], P('sec', None, 'dev'), may hold values from 0.25 to 4
- owners: int32 [32, 64, 1], P('dev', 'sec'), may hold values from 0 to 31; in each aligned block of 16 rows (0 to 15, 16 to 31, ..., all dimensions but the last counted through in order) at most 2 rows name the same one
- targets: int32 [32, 64], P('dev', 'sec'), may hold values from 0 to 15
- shell_load: float32 [6, 262144], P(None, ('sec', 'dev')), may hold values from -6 to 6
- shell_state: float32 [6, 262144], P(None, ('sec', 'dev')), may hold values from -3 to 3
- shell_inverse: float32 [6, 6, 262144], P(None, None, ('sec', 'dev')), may hold values from -0.06 to 0.5
Outputs:
- velocity_out: float32 [3, 64, 64, 4096], P(None, 'sec', None, 'dev')
- shell_out: float32 [6, 262144], P(None, ('sec', 'dev'))
Inputs may be any that keep to these rules, and one draw needn't show every extreme that they name: `owners`: among the face blocks of one device (the aligned blocks of 16 rows), no owner is named more than 2 times, a bound that some block reaches.
All inputs are finite; a program needn't handle non-finite values.
Results may differ from a plain program's by a relative error of at most 0.00013.
Values sent between devices are 32-bit elements; how exact they have to be, the bound alone decides.
A program may use at most 128 MiB of HBM per device.

v0:
```python
import jax
import jax.numpy as jnp
from jax import lax
from jax.sharding import PartitionSpec as P

SWEEPS = 8
SHELL_SWEEPS = 8
SUBITERS = 2


def with_halo(block, sides, width):
    for axis, dim in sides:
        count = lax.axis_size(axis)
        forward = [(i, i + 1) for i in range(count - 1)]
        backward = [(target, source) for source, target in forward]
        low = lax.ppermute(
            lax.slice_in_dim(block, block.shape[dim] - width, None, axis=dim), axis, forward
        )
        high = lax.ppermute(lax.slice_in_dim(block, 0, width, axis=dim), axis, backward)
        block = jnp.concatenate([low, block, high], axis=dim)
    return block


def face_terms(padded):
    inner = padded[1:-1, :, 1:-1]
    edge = jnp.pad(inner, ((0, 0), (1, 1), (0, 0)), mode="edge")
    fxm = 0.5 * (inner + padded[:-2, :, 1:-1])
    fxp = 0.5 * (inner + padded[2:, :, 1:-1])
    fzm = 0.5 * (inner + padded[1:-1, :, :-2])
    fzp = 0.5 * (inner + padded[1:-1, :, 2:])
    fym = 0.5 * (inner + edge[:, :-2, :])
    fyp = 0.5 * (inner + edge[:, 2:, :])
    denom = 1.0 + fxm + fxp + fzm + fzp + fym + fyp
    return (fxm, fxp, fzm, fzp, fym, fyp, denom)


def relax(upad, terms, rhs, wall):
    fxm, fxp, fzm, fzp, fym, fyp, denom = terms
    inner = upad[:, 1:-1, :, 1:-1]
    zero_layer = jnp.zeros((3, inner.shape[1], 1, inner.shape[3]), jnp.float32)
    uy = jnp.concatenate([wall[:, :, None, :], inner, zero_layer], axis=2)
    num = rhs + fxm * upad[:, :-2, :, 1:-1] + fxp * upad[:, 2:, :, 1:-1]
    num = num + fzm * upad[:, 1:-1, :, :-2] + fzp * upad[:, 1:-1, :, 2:]
    num = num + fym * uy[:, :, :-2, :] + fyp * uy[:, :, 2:, :]
    return num / denom


def to_rows(fields, count):
    return fields.reshape(3, count, 128).transpose(1, 0, 2).reshape(count, 384)


def from_rows(rows, count):
    return rows.reshape(count, 3, 128).transpose(1, 0, 2)


def body(velocity, source, viscosity, owners, targets, shell_load, shell_state, shell_inverse):
    cx = velocity.shape[1]
    ndev = lax.axis_size("dev")
    cap = max(2, 2 * cx // ndev)
    slots = ndev * cap
    nblocks = shell_state.shape[1] // 128
    highest = lax.Precision.HIGHEST
    owner_row = owners.reshape(cx)
    target_row = targets.reshape(cx)
    positions = jnp.arange(cx, dtype=jnp.int32)
    before = positions[None, :] < positions[:, None]
    same = owner_row[:, None] == owner_row[None, :]
    rank = jnp.sum(jnp.where(same & before, 1, 0), axis=1).astype(jnp.int32)
    slot = owner_row * cap + rank
    chosen = jnp.arange(slots, dtype=jnp.int32)[:, None] == slot[None, :]
    picker = chosen.astype(jnp.float32)
    sent_ids = jnp.sum(jnp.where(chosen, target_row[None, :] + 1, 0), axis=1) - 1
    got_ids = lax.all_to_all(
        sent_ids.reshape(ndev, cap), "dev", split_axis=0, concat_axis=0, tiled=True
    ).reshape(slots)
    loader = (jnp.arange(nblocks, dtype=jnp.int32)[:, None] == got_ids[None, :]).astype(jnp.float32)
    nu_pad = with_halo(viscosity, (("sec", 0), ("dev", 2)), 1)
    inner_terms = face_terms(nu_pad)
    u = velocity
    shell = shell_state
    for outer in range(SUBITERS):
        blocks = to_rows(shell[:3], nblocks)
        every = lax.all_gather(blocks, "dev", axis=0, tiled=True)
        wanted = owner_row * nblocks + target_row
        selector = (jnp.arange(ndev * nblocks, dtype=jnp.int32)[None, :] == wanted[:, None]).astype(
            jnp.float32
        )
        wall_rows = jnp.dot(selector, every, precision=highest, preferred_element_type=jnp.float32)
        wall = from_rows(wall_rows, cx)

        def sweep(step, state):
            upad = with_halo(state, (("sec", 1), ("dev", 3)), 1)
            return relax(upad, inner_terms, source, wall)

        u = lax.fori_loop(0, SWEEPS, sweep, u)
        traction = 2.0 * viscosity[None, :, 0, :] * (u[:, :, 0, :] - wall)
        packed = jnp.dot(
            picker, to_rows(traction, cx), precision=highest, preferred_element_type=jnp.float32
        )
        arrived = lax.all_to_all(
            packed.reshape(ndev, cap, 384), "dev", split_axis=0, concat_axis=0, tiled=True
        ).reshape(slots, 384)
        summed = jnp.dot(loader, arrived, precision=highest, preferred_element_type=jnp.float32)
        added = from_rows(summed, nblocks).reshape(3, nblocks * 128)
        force = jnp.concatenate([shell_load[:3] + added, shell_load[3:]], axis=0)

        def shell_sweep(step, state):
            padded = with_halo(state, (("dev", 1),), 1)
            drive = force + 0.4 * (padded[:, :-2] + padded[:, 2:])
            return jnp.sum(shell_inverse * drive[None, :, :], axis=1)

        shell = lax.fori_loop(0, SHELL_SWEEPS, shell_sweep, shell)
    return (u, shell)


def solution(mesh):
    in_specs = (
        P(None, "sec", None, "dev"),
        P(None, "sec", None, "dev"),
        P("sec", None, "dev"),
        P("dev", "sec", None),
        P("dev", "sec"),
        P(None, ("sec", "dev")),
        P(None, ("sec", "dev")),
        P(None, None, ("sec", "dev")),
    )
    out_specs = (P(None, "sec", None, "dev"), P(None, ("sec", "dev")))
    return jax.shard_map(body, mesh=mesh, in_specs=in_specs, out_specs=out_specs, check_vma=False)
```

profile of v0, /device:TPU:8, one launch (start us, length us, event | category | flops | bytes accessed | tf_op | source)
XLA Modules:
  0.0 859.0 jit_solution(4478846307884870364)
XLA Ops:
  10.7 8.6 %all-to-all-start = ((s32[32,1,2]{2,1,0:T(1,128)}), s32[32,1,2]{2,1,0:T(1,128)}, u32[]{:S(2)}, u32[]{:S(2)}) async-start(s32[32,1,2]{2,1,0:T(1,128)} %bitcast.8), calls=%async_computation | async-start | bytes 32768 | tf_op jit(solution)/shard_map/all_to_all | solution.py:73
  20.2 24.6 %all_gather.6 = f32[512,384]{1,0:T(8,128)S(1)} all-gather(f32[16,384]{1,0:T(8,128)S(1)} %bitcast.95), channel_id=1, replica_groups=mesh['sec'=4,'dev'=32] {'dev'}, dimensions={0}, use_global_device_ids=true | all-gather | bytes 811008 | tf_op jit(solution)/shard_map/all_gather | solution.py:83
  47.5 5.4 collective-permute-start.15
  64.8 278.3 %while.40 = (s32[]{:T(128)}, f32[3,16,64,128]{2,3,1,0:T(8,128)}, f32[16,64,128]{1,2,0:T(8,128)}, f32[3,16,64,128]{2,3,1,0:T(8,128)}, f32[16,64,128]{1,2,0:T(8,12...) while((s32[]{:T(128)}, f32[3,16,64,128]{2,3,1,0:T(8,128)}, ...), condition=%wide.region_1.2_spmd, body=%wide.region_0.1_spmd.sunk | while | flops 7077890 | bytes 29005104 | solution.py:95
  90.8 10.6 %fusion.102 = f32[3,16,64,128]{2,3,1,0:T(8,128)} fusion(f32[3,16,64,128]{2,3,1,0:T(8,128)S(1)} %copy.178, f32[3,16,1,128]{2,3,1,0:T(8,128)} %copy.142, f32[3,18,64,1]{2,3,1,0:T(1,128)} %collective-permute-done.2, f32[3,18,64,128]{2,3,1,0:T(8,128)} %copy-done.1, f32[3,18,64,1]{2,3,1,0:T(1,128)} %collective-permute-done.3, ...), kind=kLoop, calls=%fused_computation.4.clone.1 | loop fusion | flops 7077888 | bytes 10406912 | tf_op jit(solution)/shard_map/while/body/eval_jaxpr/div | solution.py:45
  127.0 10.6 %fusion.102 = f32[3,16,64,128]{2,3,1,0:T(8,128)} fusion(f32[3,16,64,128]{2,3,1,0:T(8,128)S(1)} %copy.178, f32[3,16,1,128]{2,3,1,0:T(8,128)} %copy.142, f32[3,18,64,1]{2,3,1,0:T(1,128)} %collective-permute-done.2, f32[3,18,64,128]{2,3,1,0:T(8,128)} %copy-done.1, f32[3,18,64,1]{2,3,1,0:T(1,128)} %collective-permute-done.3, ...), kind=kLoop, calls=%fused_computation.4.clone.1 | loop fusion | flops 7077888 | bytes 10406912 | tf_op jit(solution)/shard_map/while/body/eval_jaxpr/div | solution.py:45
  162.2 10.6 %fusion.102 = f32[3,16,64,128]{2,3,1,0:T(8,128)} fusion(f32[3,16,64,128]{2,3,1,0:T(8,128)S(1)} %copy.178, f32[3,16,1,128]{2,3,1,0:T(8,128)} %copy.142, f32[3,18,64,1]{2,3,1,0:T(1,128)} %collective-permute-done.2, f32[3,18,64,128]{2,3,1,0:T(8,128)} %copy-done.1, f32[3,18,64,1]{2,3,1,0:T(1,128)} %collective-permute-done.3, ...), kind=kLoop, calls=%fused_computation.4.clone.1 | loop fusion | flops 7077888 | bytes 10406912 | tf_op jit(solution)/shard_map/while/body/eval_jaxpr/div | solution.py:45
  196.4 10.6 %fusion.102 = f32[3,16,64,128]{2,3,1,0:T(8,128)} fusion(f32[3,16,64,128]{2,3,1,0:T(8,128)S(1)} %copy.178, f32[3,16,1,128]{2,3,1,0:T(8,128)} %copy.142, f32[3,18,64,1]{2,3,1,0:T(1,128)} %collective-permute-done.2, f32[3,18,64,128]{2,3,1,0:T(8,128)} %copy-done.1, f32[3,18,64,1]{2,3,1,0:T(1,128)} %collective-permute-done.3, ...), kind=kLoop, calls=%fused_computation.4.clone.1 | loop fusion | flops 7077888 | bytes 10406912 | tf_op jit(solution)/shard_map/while/body/eval_jaxpr/div | solution.py:45
  230.4 10.6 %fusion.102 = f32[3,16,64,128]{2,3,1,0:T(8,128)} fusion(f32[3,16,64,128]{2,3,1,0:T(8,128)S(1)} %copy.178, f32[3,16,1,128]{2,3,1,0:T(8,128)} %copy.142, f32[3,18,64,1]{2,3,1,0:T(1,128)} %collective-permute-done.2, f32[3,18,64,128]{2,3,1,0:T(8,128)} %copy-done.1, f32[3,18,64,1]{2,3,1,0:T(1,128)} %collective-permute-done.3, ...), kind=kLoop, calls=%fused_computation.4.clone.1 | loop fusion | flops 7077888 | bytes 10406912 | tf_op jit(solution)/shard_map/while/body/eval_jaxpr/div | solution.py:45
  264.4 10.6 %fusion.102 = f32[3,16,64,128]{2,3,1,0:T(8,128)} fusion(f32[3,16,64,128]{2,3,1,0:T(8,128)S(1)} %copy.178, f32[3,16,1,128]{2,3,1,0:T(8,128)} %copy.142, f32[3,18,64,1]{2,3,1,0:T(1,128)} %collective-permute-done.2, f32[3,18,64,128]{2,3,1,0:T(8,128)} %copy-done.1, f32[3,18,64,1]{2,3,1,0:T(1,128)} %collective-permute-done.3, ...), kind=kLoop, calls=%fused_computation.4.clone.1 | loop fusion | flops 7077888 | bytes 10406912 | tf_op jit(solution)/shard_map/while/body/eval_jaxpr/div | solution.py:45
  298.4 10.6 %fusion.102 = f32[3,16,64,128]{2,3,1,0:T(8,128)} fusion(f32[3,16,64,128]{2,3,1,0:T(8,128)S(1)} %copy.178, f32[3,16,1,128]{2,3,1,0:T(8,128)} %copy.142, f32[3,18,64,1]{2,3,1,0:T(1,128)} %collective-permute-done.2, f32[3,18,64,128]{2,3,1,0:T(8,128)} %copy-done.1, f32[3,18,64,1]{2,3,1,0:T(1,128)} %collective-permute-done.3, ...), kind=kLoop, calls=%fused_computation.4.clone.1 | loop fusion | flops 7077888 | bytes 10406912 | tf_op jit(solution)/shard_map/while/body/eval_jaxpr/div | solution.py:45
  332.5 10.6 %fusion.102 = f32[3,16,64,128]{2,3,1,0:T(8,128)} fusion(f32[3,16,64,128]{2,3,1,0:T(8,128)S(1)} %copy.178, f32[3,16,1,128]{2,3,1,0:T(8,128)} %copy.142, f32[3,18,64,1]{2,3,1,0:T(1,128)} %collective-permute-done.2, f32[3,18,64,128]{2,3,1,0:T(8,128)} %copy-done.1, f32[3,18,64,1]{2,3,1,0:T(1,128)} %collective-permute-done.3, ...), kind=kLoop, calls=%fused_computation.4.clone.1 | loop fusion | flops 7077888 | bytes 10406912 | tf_op jit(solution)/shard_map/while/body/eval_jaxpr/div | solution.py:45
  348.1 5.0 all-to-all-start.1
  360.4 76.1 %while.41 = (s32[]{:T(128)}, f32[6,2048]{1,0:T(8,128)S(1)}, f32[6,2048]{1,0:T(8,128)S(1)}, f32[6,6,2048]{2,1,0:T(8,128)S(1)}, s32[]{:T(128)}) while((s32[]{:T(128)}, f32[6,2048]{1,0:T(8,128)S(1)}, f32[6,2048]{1,0:T(8,128)S(1)}, f32[6,6,2048]{2,1,0:T(8,128)S(1)}, s32[]{:T(128)}) %tuple.123), condition=%wide.region_6.7_spmd, body=%wide.region_4.6_spmd.sunk | while | flops 196610 | bytes 541149 | solution.py:112
  366.1 5.1 collective-permute-done.5
  375.9 4.6 collective-permute-done.5
  385.2 4.6 collective-permute-done.5
  394.4 4.6 collective-permute-done.5
  436.5 22.6 %all_gather.7 = f32[512,384]{1,0:T(8,128)S(1)} all-gather(f32[16,384]{1,0:T(8,128)S(1)} %bitcast.96), channel_id=1, replica_groups=mesh['sec'=4,'dev'=32] {'dev'}, dimensions={0}, use_global_device_ids=true | all-gather | bytes 811008 | tf_op jit(solution)/shard_map/all_gather | solution.py:83
  460.1 281.1 %while.42 = (s32[]{:T(128)}, f32[3,16,64,128]{2,3,1,0:T(8,128)}, f32[16,64,128]{1,2,0:T(8,128)}, f32[3,16,64,128]{2,3,1,0:T(8,128)}, f32[16,64,128]{1,2,0:T(8,12...) while((s32[]{:T(128)}, f32[3,16,64,128]{2,3,1,0:T(8,128)}, ...), condition=%wide.region_8.9_spmd, body=%wide.region_7.8_spmd.sunk | while | flops 7077890 | bytes 29791592 | solution.py:95
  485.6 11.3 %fusion.107 = f32[3,16,64,128]{2,3,1,0:T(8,128)} fusion(f32[3,16,64,128]{2,3,1,0:T(8,128)S(1)} %copy.179, f32[3,16,1,128]{2,3,1,0:T(8,128)} %copy.143, f32[3,18,64,1]{2,3,1,0:T(1,128)} %collective-permute-done.8, f32[3,18,64,128]{2,3,1,0:T(8,128)} %copy-done.2, f32[3,18,64,1]{2,3,1,0:T(1,128)} %collective-permute-done.9, ...), kind=kLoop, calls=%fused_computation.30.clone.1 | loop fusion | flops 7077888 | bytes 10406912 | tf_op jit(solution)/shard_map/while/body/eval_jaxpr/div | solution.py:45
  521.2 11.3 %fusion.107 = f32[3,16,64,128]{2,3,1,0:T(8,128)} fusion(f32[3,16,64,128]{2,3,1,0:T(8,128)S(1)} %copy.179, f32[3,16,1,128]{2,3,1,0:T(8,128)} %copy.143, f32[3,18,64,1]{2,3,1,0:T(1,128)} %collective-permute-done.8, f32[3,18,64,128]{2,3,1,0:T(8,128)} %copy-done.2, f32[3,18,64,1]{2,3,1,0:T(1,128)} %collective-permute-done.9, ...), kind=kLoop, calls=%fused_computation.30.clone.1 | loop fusion | flops 7077888 | bytes 10406912 | tf_op jit(solution)/shard_map/while/body/eval_jaxpr/div | solution.py:45
  556.0 11.3 %fusion.107 = f32[3,16,64,128]{2,3,1,0:T(8,128)} fusion(f32[3,16,64,128]{2,3,1,0:T(8,128)S(1)} %copy.179, f32[3,16,1,128]{2,3,1,0:T(8,128)} %copy.143, f32[3,18,64,1]{2,3,1,0:T(1,128)} %collective-permute-done.8, f32[3,18,64,128]{2,3,1,0:T(8,128)} %copy-done.2, f32[3,18,64,1]{2,3,1,0:T(1,128)} %collective-permute-done.9, ...), kind=kLoop, calls=%fused_computation.30.clone.1 | loop fusion | flops 7077888 | bytes 10406912 | tf_op jit(solution)/shard_map/while/body/eval_jaxpr/div | solution.py:45
  590.9 11.3 %fusion.107 = f32[3,16,64,128]{2,3,1,0:T(8,128)} fusion(f32[3,16,64,128]{2,3,1,0:T(8,128)S(1)} %copy.179, f32[3,16,1,128]{2,3,1,0:T(8,128)} %copy.143, f32[3,18,64,1]{2,3,1,0:T(1,128)} %collective-permute-done.8, f32[3,18,64,128]{2,3,1,0:T(8,128)} %copy-done.2, f32[3,18,64,1]{2,3,1,0:T(1,128)} %collective-permute-done.9, ...), kind=kLoop, calls=%fused_computation.30.clone.1 | loop fusion | flops 7077888 | bytes 10406912 | tf_op jit(solution)/shard_map/while/body/eval_jaxpr/div | solution.py:45
  625.6 11.3 %fusion.107 = f32[3,16,64,128]{2,3,1,0:T(8,128)} fusion(f32[3,16,64,128]{2,3,1,0:T(8,128)S(1)} %copy.179, f32[3,16,1,128]{2,3,1,0:T(8,128)} %copy.143, f32[3,18,64,1]{2,3,1,0:T(1,128)} %collective-permute-done.8, f32[3,18,64,128]{2,3,1,0:T(8,128)} %copy-done.2, f32[3,18,64,1]{2,3,1,0:T(1,128)} %collective-permute-done.9, ...), kind=kLoop, calls=%fused_computation.30.clone.1 | loop fusion | flops 7077888 | bytes 10406912 | tf_op jit(solution)/shard_map/while/body/eval_jaxpr/div | solution.py:45
  660.4 11.3 %fusion.107 = f32[3,16,64,128]{2,3,1,0:T(8,128)} fusion(f32[3,16,64,128]{2,3,1,0:T(8,128)S(1)} %copy.179, f32[3,16,1,128]{2,3,1,0:T(8,128)} %copy.143, f32[3,18,64,1]{2,3,1,0:T(1,128)} %collective-permute-done.8, f32[3,18,64,128]{2,3,1,0:T(8,128)} %copy-done.2, f32[3,18,64,1]{2,3,1,0:T(1,128)} %collective-permute-done.9, ...), kind=kLoop, calls=%fused_computation.30.clone.1 | loop fusion | flops 7077888 | bytes 10406912 | tf_op jit(solution)/shard_map/while/body/eval_jaxpr/div | solution.py:45
  695.2 11.3 %fusion.107 = f32[3,16,64,128]{2,3,1,0:T(8,128)} fusion(f32[3,16,64,128]{2,3,1,0:T(8,128)S(1)} %copy.179, f32[3,16,1,128]{2,3,1,0:T(8,128)} %copy.143, f32[3,18,64,1]{2,3,1,0:T(1,128)} %collective-permute-done.8, f32[3,18,64,128]{2,3,1,0:T(8,128)} %copy-done.2, f32[3,18,64,1]{2,3,1,0:T(1,128)} %collective-permute-done.9, ...), kind=kLoop, calls=%fused_computation.30.clone.1 | loop fusion | flops 7077888 | bytes 10406912 | tf_op jit(solution)/shard_map/while/body/eval_jaxpr/div | solution.py:45
  730.0 11.3 %fusion.107 = f32[3,16,64,128]{2,3,1,0:T(8,128)} fusion(f32[3,16,64,128]{2,3,1,0:T(8,128)S(1)} %copy.179, f32[3,16,1,128]{2,3,1,0:T(8,128)} %copy.143, f32[3,18,64,1]{2,3,1,0:T(1,128)} %collective-permute-done.8, f32[3,18,64,128]{2,3,1,0:T(8,128)} %copy-done.2, f32[3,18,64,1]{2,3,1,0:T(1,128)} %collective-permute-done.9, ...), kind=kLoop, calls=%fused_computation.30.clone.1 | loop fusion | flops 7077888 | bytes 10406912 | tf_op jit(solution)/shard_map/while/body/eval_jaxpr/div | solution.py:45
  741.3 4.7 copy.115
  750.5 5.4 all-to-all-start.2
  765.2 93.9 %while.43 = (s32[]{:T(128)}, f32[6,2048]{1,0:T(8,128)}, f32[6,2048]{1,0:T(8,128)S(1)}, f32[6,6,2048]{2,1,0:T(8,128)S(1)}, s32[]{:T(128)}) while((s32[]{:T(128)}, f32[6,2048]{1,0:T(8,128)}, f32[6,2048]{1,0:T(8,128)S(1)}, f32[6,6,2048]{2,1,0:T(8,128)S(1)}, s32[]{:T(128)}) %tuple.124), condition=%wide.region_11.12_spmd, body=%wide.region_9.11_spmd.sunk | while | flops 196610 | bytes 541149 | solution.py:112
  771.6 5.1 collective-permute-done.11
  (496 shorter events, 580.3 us)
Async XLA Ops:
  2.9 42.3 %collective-permute-start.12 = (f32[1,64,128]{1,2,0:T(8,128)S(1)}, f32[1,64,128]{1,2,0:T(8,128)S(1)}, u32[]{:S(2)}, u32[]{:S(2)}) collective-permute-start(f32[1,64,128]{1,2,0:T(8,128)S(1)} %get-tuple-element.339), channel_id=1, source_target_pairs={{0,32},{32,64},{64,96},{1,33},{33,65},{65,97},{2,34},{34,66},{66,9... | collective-permute-start | bytes 98312 | tf_op jit(solution)/shard_map/ppermute | solution.py:16
  6.3 38.9 %collective-permute-start.13 = (f32[1,64,128]{1,2,0:T(8,128)S(1)}, f32[1,64,128]{1,2,0:T(8,128)S(1)}, u32[]{:S(2)}, u32[]{:S(2)}) collective-permute-start(f32[1,64,128]{1,2,0:T(8,128)S(1)} %get-tuple-element.340), channel_id=1, source_target_pairs={{32,0},{64,32},{96,64},{33,1},{65,33},{97,65},{34,2},{66,34},{98,6... | collective-permute-start | bytes 98312 | tf_op jit(solution)/shard_map/ppermute | solution.py:19
  10.7 337.4 %all-to-all-start = ((s32[32,1,2]{2,1,0:T(1,128)}), s32[32,1,2]{2,1,0:T(1,128)}, u32[]{:S(2)}, u32[]{:S(2)}) async-start(s32[32,1,2]{2,1,0:T(1,128)} %bitcast.8), calls=%async_computation | async-start | bytes 32768 | tf_op jit(solution)/shard_map/all_to_all | solution.py:73
  45.2 15.7 %collective-permute-start.14 = (f32[18,64,1]{1,2,0:T(1,128)S(1)}, f32[18,64,1]{1,2,0:T(1,128)S(1)}, u32[]{:S(2)}, u32[]{:S(2)}) collective-permute-start(f32[18,64,1]{1,2,0:T(1,128)S(1)} %get-tuple-element.337), channel_id=1, source_target_pairs={{0,1},{1,2},{2,3},{3,4},{4,5},{5,6},{6,7},{7,8},{8,9},{9,10},{10,1... | collective-permute-start | bytes 13832 | tf_op jit(solution)/shard_map/ppermute | solution.py:16
  47.5 13.5 %collective-permute-start.15 = (f32[18,64,1]{1,2,0:T(1,128)S(1)}, f32[18,64,1]{1,2,0:T(1,128)S(1)}, u32[]{:S(2)}, u32[]{:S(2)}) collective-permute-start(f32[18,64,1]{1,2,0:T(1,128)S(1)} %get-tuple-element.338), channel_id=1, source_target_pairs={{1,0},{2,1},{3,2},{4,3},{5,4},{6,5},{7,6},{8,7},{9,8},{10,9},{11,1... | collective-permute-start | bytes 13832 | tf_op jit(solution)/shard_map/ppermute | solution.py:19
  66.8 7.7 collective-permute-start
  71.3 7.6 collective-permute-start.1
  83.2 7.6 collective-permute-start.3
  106.8 7.6 collective-permute-start.1
  119.4 7.6 collective-permute-start.3
  142.7 7.6 collective-permute-start.1
  154.6 7.6 collective-permute-start.3
  176.9 7.6 collective-permute-start.1
  188.8 7.6 collective-permute-start.3
  222.8 7.6 collective-permute-start.3
  256.8 7.6 collective-permute-start.3
  290.8 7.6 collective-permute-start.3
  324.9 7.6 collective-permute-start.3
  348.1 11.4 %all-to-all-start.1 = ((f32[32,2,384]{2,1,0:T(2,128)}), f32[32,2,384]{2,1,0:T(2,128)S(1)}, u32[]{:S(2)}, u32[]{:S(2)}) async-start(f32[32,2,384]{2,1,0:T(2,128)} %copy.110), calls=%async_computation.1 | async-start | bytes 196608 | tf_op jit(solution)/shard_map/all_to_all | solution.py:100
  464.0 8.8 %collective-permute-start.7 = (f32[3,1,64,128]{2,3,1,0:T(8,128)S(1)}, f32[3,1,64,128]{2,3,1,0:T(8,128)S(1)}, u32[]{:S(2)}, u32[]{:S(2)}) collective-permute-start(f32[3,1,64,128]{2,3,1,0:T(8,128)S(1)} %get-tuple-element.546), channel_id=1, source_target_pairs={{32,0},{64,32},{96,64},{33,1},{65,33},{97,65},{34,2},{66,34},{98,6... | collective-permute-start | bytes 294920 | tf_op jit(solution)/shard_map/while/body/eval_jaxpr/ppermute | solution.py:19
  475.2 7.7 collective-permute-start.8
  478.0 7.6 collective-permute-start.9
  513.6 7.6 collective-permute-start.9
  536.4 7.6 collective-permute-start.7
  548.4 7.6 collective-permute-start.9
  583.3 7.6 collective-permute-start.9
  618.0 7.6 collective-permute-start.9
  640.8 7.6 collective-permute-start.7
  652.7 7.6 collective-permute-start.9
  687.6 7.6 collective-permute-start.9
  722.3 7.6 collective-permute-start.9
  750.5 11.9 %all-to-all-start.2 = ((f32[32,2,384]{2,1,0:T(2,128)}), f32[32,2,384]{2,1,0:T(2,128)}, u32[]{:S(2)}, u32[]{:S(2)}) async-start(f32[32,2,384]{2,1,0:T(2,128)} %copy.116), calls=%async_computation.2 | async-start | bytes 196608 | tf_op jit(solution)/shard_map/all_to_all | solution.py:100
  (116 other events, 1090.7 us)
where the time goes:
time: 865 us; the launch traced here: 859 us
  starting transfers between devices  230 us (27%)
  waiting for transfers between devices  214 us (25%)
  other arithmetic  202 us (23%)
  local copies, waits for them, and re-layouts  160 us (18%)
  blocking collectives  47.2 us (5%)
    div x16, other arithmetic, relax(): return num / denom  176 us
    ppermute x50, waiting for transfers between devices, with_halo(): lax.ppermute(lax.slice_in_dim(block, block.shape[dim] - width, None, axis...  144 us
    ppermute x50, starting transfers between devices, with_halo(): lax.ppermute(lax.slice_in_dim(block, block.shape[dim] - width, None, axis...  117 us
    ppermute x50, starting transfers between devices, with_halo(): lax.ppermute(lax.slice_in_dim(block, 0, width, axis=dim), axis, backward)  94.3 us
    while x112, local copies, waits for them, and re-layouts  67.3 us
    ppermute x50, waiting for transfers between devices, with_halo(): lax.ppermute(lax.slice_in_dim(block, 0, width, axis=dim), axis, backward)  61.1 us
    all_gather x2, blocking collectives, body(): every = lax.all_gather(blocks, 'dev', axis=0, tiled=True)  47.2 us
    broadcast_in_dim x16, local copies, waits for them, and re-layouts, relax(): uy = jnp.concatenate([wall[:, :, None, :], inner, zero_layer], axis=2)  46.9 us
  transfers between devices with their start and end apart: 103, of which 66 were waited for; matrix products, arithmetic and copies ran while one was open for 21% of the time, Pallas kernels for 0%

commit v1 on v0

v1 whole, which is shorter than its diff:
```python
import jax
import jax.numpy as jnp
from jax import lax
from jax.experimental import pallas as pl
from jax.experimental.pallas import tpu as pltpu
from jax.sharding import PartitionSpec as P

SWEEPS = 8
SHELL_SWEEPS = 8
SUBITERS = 2
CX = 16
NY = 64
LANES = 128
NB = 16
ROWS = 3 * CX
MESH = pl.DeviceIdType.MESH
F32 = jnp.float32
HIGHEST = lax.Precision.HIGHEST


def kernel(
    nsec, ndev,
    vel_ref, src_ref, nu_ref, key_ref, tgt_ref, load_ref, state_ref, inv_ref,
    uout_ref, sout_ref,
    U, NU, CF, RHS, ZS, ZR, MV, NZS, NZR,
    S, ST, G, GT, AS, AR, WROW, WALL,
    SH, FORCE, INV, IS, IR, HS, HR,
    xs_sem, xr_sem, zs_sem, zr_sem, nxs_sem, nxr_sem, nzs_sem, nzr_sem,
    as_sem, ar_sem, is_sem, ir_sem, hs_sem, hr_sem,
):
    sec = lax.axis_index("sec")
    dev = lax.axis_index("dev")
    has = {("x", 0): sec > 0, ("x", 1): sec < nsec - 1, ("z", 0): dev > 0, ("z", 1): dev < ndev - 1}
    lane = lax.broadcasted_iota(jnp.int32, (8, LANES), 1)
    sub = lax.broadcasted_iota(jnp.int32, (8, LANES), 0)

    def target(axis, side):
        step = 1 if side else -1
        return {"sec": sec + step} if axis == "x" else {"dev": dev + step}

    def u_copy(slot, c, side):
        own, there = (CX, 0) if side else (1, CX + 1)
        return pltpu.make_async_remote_copy(
            src_ref=U.at[slot, c, own], dst_ref=U.at[slot, c, there],
            send_sem=xs_sem.at[slot, c, side], recv_sem=xr_sem.at[slot, c, 1 - side],
            device_id=target("x", side), device_id_type=MESH)

    def z_copy(slot, c, side):
        return pltpu.make_async_remote_copy(
            src_ref=ZS.at[slot, c], dst_ref=ZR.at[slot, c, 1 - side],
            send_sem=zs_sem.at[slot, c, side], recv_sem=zr_sem.at[slot, c, 1 - side],
            device_id=target("z", side), device_id_type=MESH)

    def nu_copy(side):
        own, there = (CX, 0) if side else (1, CX + 1)
        return pltpu.make_async_remote_copy(
            src_ref=NU.at[own], dst_ref=NU.at[there],
            send_sem=nxs_sem.at[side], recv_sem=nxr_sem.at[1 - side],
            device_id=target("x", side), device_id_type=MESH)

    def nz_copy(side):
        return pltpu.make_async_remote_copy(
            src_ref=NZS, dst_ref=NZR.at[1 - side],
            send_sem=nzs_sem.at[side], recv_sem=nzr_sem.at[1 - side],
            device_id=target("z", side), device_id_type=MESH)

    def inv_copy(side):
        return pltpu.make_async_remote_copy(
            src_ref=IS.at[side], dst_ref=IR.at[1 - side],
            send_sem=is_sem.at[side], recv_sem=ir_sem.at[1 - side],
            device_id=target("z", side), device_id_type=MESH)

    def end_copy(k, side):
        return pltpu.make_async_remote_copy(
            src_ref=HS.at[k, side], dst_ref=HR.at[k, 1 - side],
            send_sem=hs_sem.at[k, side], recv_sem=hr_sem.at[k, 1 - side],
            device_id=target("z", side), device_id_type=MESH)

    def both(axis, act):
        for side in (0, 1):
            @pl.when(has[(axis, side)])
            def _():
                act(side)

    def exchange_start(phase):
        def send(i, carry):
            peer = lax.rem(dev + i, ndev)
            pltpu.make_async_remote_copy(
                src_ref=AS.at[phase, peer], dst_ref=AR.at[phase, dev],
                send_sem=as_sem.at[phase], recv_sem=ar_sem.at[phase],
                device_id={"dev": peer}, device_id_type=MESH).start()
            return carry

        lax.fori_loop(1, ndev, send, 0)
        AR[phase, dev] = AS[phase, dev]

    def exchange_wait(phase):
        copy = pltpu.make_async_remote_copy(
            src_ref=AS.at[phase, pl.ds(0, ndev - 1)], dst_ref=AR.at[phase, pl.ds(0, ndev - 1)],
            send_sem=as_sem.at[phase], recv_sem=ar_sem.at[phase],
            device_id={"dev": lax.rem(dev + 1, ndev)}, device_id_type=MESH)
        copy.wait_send()
        copy.wait_recv()

    def dot(a, b):
        return lax.dot_general(a, b, (((1,), (0,)), ((), ())), precision=HIGHEST, preferred_element_type=F32)

    def tall(rows):
        return jnp.concatenate([rows, jnp.zeros((LANES - ROWS, LANES), F32)], axis=0)

    def pack_plane(ref, x, tiles):
        packed = tiles[0]
        for j in range(1, 8):
            packed = jnp.where((lane == 2 * j) | (lane == 2 * j - 1), pltpu.roll(tiles[j], 2 * j, 1), packed)
        m = lax.rem(x, 8)
        packed = pltpu.roll(packed, 16 * m, 1)
        here = lax.rem(lane + 1, LANES) // 16 == m
        v = x // 8
        ref[v] = jnp.where(here, packed, ref[v])

    def merged(low, high):
        return jnp.where(lane % 2 == 0, pltpu.roll(low, 1, 1), pltpu.roll(high, LANES - 1, 1))

    def z_pair(tile, mx, j):
        h = pltpu.roll(mx, (LANES - 2 * j) % LANES, 1)
        zm = jnp.where(lane == 0, h, pltpu.roll(tile, 1, 1))
        zp = jnp.where(lane == LANES - 1, h, pltpu.roll(tile, LANES - 1, 1))
        return zm, zp

    def halo_row(x):
        return pltpu.roll(MV[x // 8], lax.rem(LANES - 16 * lax.rem(x, 8), LANES), 1)

    zero_plane = jnp.zeros((NY, LANES), F32)
    for slot in (0, 1):
        for c in range(3):
            U[slot, c, 0] = zero_plane
            U[slot, c, CX + 1] = zero_plane
    NU[0] = zero_plane
    NU[CX + 1] = zero_plane
    ZR[...] = jnp.zeros(ZR.shape, F32)
    ZS[...] = jnp.zeros(ZS.shape, F32)
    NZR[...] = jnp.zeros(NZR.shape, F32)
    NZS[...] = jnp.zeros(NZS.shape, F32)
    IR[...] = jnp.zeros(IR.shape, F32)
    IS[...] = jnp.zeros(IS.shape, F32)
    HR[...] = jnp.zeros(HR.shape, F32)
    HS[...] = jnp.zeros(HS.shape, F32)

    barrier = pltpu.get_barrier_semaphore()

    def greet(i, carry):
        pl.semaphore_signal(barrier, inc=1, device_id={"dev": lax.rem(dev + i, ndev)}, device_id_type=MESH)
        return carry

    lax.fori_loop(1, ndev, greet, 0)
    both("x", lambda side: pl.semaphore_signal(barrier, inc=1, device_id=target("x", side), device_id_type=MESH))

    def take(x, carry):
        tiles = []
        for j in range(8):
            tile = nu_ref[x, pl.ds(j, 8, stride=8), :]
            NU[x + 1, pl.ds(8 * j, 8), :] = tile
            tiles.append(tile)
        pack_plane(NZS, x, tiles)
        for c in range(3):
            tiles = []
            for j in range(8):
                tile = vel_ref[c, x, pl.ds(j, 8, stride=8), :]
                U[0, c, x + 1, pl.ds(8 * j, 8), :] = tile
                tiles.append(tile)
            pack_plane(ZS.at[0, c], x, tiles)
        return carry

    lax.fori_loop(0, CX, take, 0)
    rows256 = lax.broadcasted_iota(jnp.int32, (8 * ndev, LANES), 0)
    one_hot = jnp.where(rows256 == key_ref[...], 1.0, 0.0).astype(F32)
    S[...] = one_hot
    ST[...] = one_hot.T
    rows128 = lax.broadcasted_iota(jnp.int32, (LANES, LANES), 0)
    names = jnp.where(rows128 == tgt_ref[...], 1.0, 0.0).astype(F32)
    AS[0] = dot(one_hot, names.T).reshape(ndev, 8, LANES)
    for a in range(6):
        IS[0, pl.ds(6 * a, 6), :] = inv_ref[a, :, 0, :]
        IS[1, pl.ds(6 * a, 6), :] = inv_ref[a, :, NB - 1, :]

    others = (ndev - 1) + jnp.where(has[("x", 0)], 1, 0) + jnp.where(has[("x", 1)], 1, 0)
    pl.semaphore_wait(barrier, others)

    both("x", lambda side: nu_copy(side).start())
    both("z", lambda side: nz_copy(side).start())
    exchange_start(0)
    for c in range(3):
        both("x", lambda side: u_copy(0, c, side).start())
        both("z", lambda side: z_copy(0, c, side).start())
    both("z", lambda side: inv_copy(side).start())

    SH[...] = jnp.zeros(SH.shape, F32)
    FORCE[...] = jnp.zeros(FORCE.shape, F32)
    for f in range(6):
        SH[f, pl.ds(0, NB), :] = state_ref[f]

    def ends(right, left):
        return jnp.where(sub == 0, right, jnp.where(sub == 7, left, 0.0))

    exchange_wait(0)
    got = AR[0].reshape(8 * ndev, LANES)
    G[...] = got
    GT[...] = got.T

    def send_wall(k):
        rows = jnp.concatenate([SH[f, pl.ds(0, NB), :] for f in range(3)], axis=0)
        AS[1 + k] = dot(G[...], tall(rows)).reshape(ndev, 8, LANES)
        exchange_start(1 + k)

    def take_wall(k):
        exchange_wait(1 + k)
        wall = dot(ST[...], AR[1 + k].reshape(8 * ndev, LANES))
        WROW[...] = wall[:ROWS]
        for q in range(ROWS):
            WALL[q] = jnp.broadcast_to(wall[q : q + 1], (8, LANES))

    send_wall(0)

    both("x", lambda side: nu_copy(side).wait_send())
    both("x", lambda side: nu_copy(1 - side).wait_recv())
    both("z", lambda side: nz_copy(side).wait_send())
    both("z", lambda side: nz_copy(1 - side).wait_recv())
    for v in range(2):
        MV[v] = merged(NZR[0, v], NZR[1, v])

    def coefficients(x, carry):
        mx = halo_row(x)
        tiles = [NU[x + 1, pl.ds(8 * j, 8), :] for j in range(8)]
        for j in range(8):
            rows = pl.ds(8 * j, 8)
            t = tiles[j]
            zm, zp = z_pair(t, mx, j)
            ym = tiles[j - 1] if j else jnp.where(sub == 0, t, pltpu.roll(tiles[7], 1, 0))
            yp = tiles[j + 1] if j < 7 else jnp.where(sub == 7, t, pltpu.roll(tiles[0], 7, 0))
            faces = [0.5 * (t + o) for o in (NU[x, rows, :], NU[x + 2, rows, :], zm, zp, ym, yp)]
            total = 1.0 + faces[0]
            for f in faces[1:]:
                total = total + f
            inverse = 1.0 / total
            for n, f in enumerate(faces):
                CF[n, x, rows, :] = f * inverse
            for c in range(3):
                RHS[c, x, rows, :] = src_ref[c, x, pl.ds(j, 8, stride=8), :] * inverse
        return carry

    lax.fori_loop(0, CX, coefficients, 0)

    both("z", lambda side: inv_copy(side).wait_send())
    both("z", lambda side: inv_copy(1 - side).wait_recv())
    for a in range(6):
        for b in range(6):
            n = 6 * a + b
            INV[n, pl.ds(0, NB), :] = inv_ref[a, b]
            INV[n, pl.ds(NB, 8), :] = ends(IR[1, pl.ds(n, 1), :], IR[0, pl.ds(n, 1), :])

    def plane(c, x, old, new):
        mx = halo_row(x)
        tiles = [U[old, c, x + 1, pl.ds(8 * j, 8), :] for j in range(8)]
        done = []
        for j in range(8):
            rows = pl.ds(8 * j, 8)
            t = tiles[j]
            zm, zp = z_pair(t, mx, j)
            ym = tiles[j - 1] if j else jnp.where(sub == 0, WALL[c * CX + x], pltpu.roll(tiles[7], 1, 0))
            yp = tiles[j + 1] if j < 7 else jnp.where(sub == 7, 0.0, pltpu.roll(tiles[0], 7, 0))
            num = RHS[c, x, rows, :] + CF[0, x, rows, :] * U[old, c, x, rows, :]
            num = num + CF[1, x, rows, :] * U[old, c, x + 2, rows, :]
            num = num + CF[2, x, rows, :] * zm + CF[3, x, rows, :] * zp
            num = num + CF[4, x, rows, :] * ym + CF[5, x, rows, :] * yp
            U[new, c, x + 1, rows, :] = num
            done.append(num)
        pack_plane(ZS.at[new, c], x, done)

    last = SUBITERS * SWEEPS

    def level(k, carry):
        new = lax.rem(k, 2)
        old = 1 - new

        def component(c, carry):
            both("z", lambda side: z_copy(old, c, 1 - side).wait_recv())
            for v in range(2):
                MV[v] = merged(ZR[old, c, 0, v], ZR[old, c, 1, v])
            both("x", lambda side: u_copy(old, c, 1 - side).wait_recv())

            @pl.when(k >= 2)
            def _():
                both("x", lambda side: u_copy(new, c, side).wait_send())
                both("z", lambda side: z_copy(new, c, side).wait_send())

            def edge(i, carry):
                plane(c, i * (CX - 1), old, new)
                return carry

            lax.fori_loop(0, 2, edge, 0)

            @pl.when(k < last)
            def _():
                both("x", lambda side: u_copy(new, c, side).start())

            def inner(x, carry):
                plane(c, x, old, new)
                return carry

            lax.fori_loop(1, CX - 1, inner, 0)

            @pl.when(k < last)
            def _():
                both("z", lambda side: z_copy(new, c, side).start())
            return carry

        lax.fori_loop(0, 3, component, 0)
        return carry

    def shell_sweep(step, carry):
        drive = []
        lane24 = lax.broadcasted_iota(jnp.int32, (24, LANES), 1)
        for f in range(6):
            s = SH[f]
            up = pltpu.roll(s, 1, 1)
            before = jnp.where(lane24 == 0, pltpu.roll(up, 1, 0), up)
            down = pltpu.roll(s, LANES - 1, 1)
            after = jnp.where(lane24 == LANES - 1, pltpu.roll(down, 23, 0), down)
            drive.append(FORCE[f] + 0.4 * (before + after))
        for a in range(6):
            total = INV[6 * a] * drive[0]
            for b in range(1, 6):
                total = total + INV[6 * a + b] * drive[b]
            SH[a] = total
        return carry

    def subiteration(k, carry):
        take_wall(k)
        lax.fori_loop(k * SWEEPS + 1, (k + 1) * SWEEPS + 1, level, 0)
        double = 2.0 * NU[pl.ds(1, CX), 0, :]
        pulls = []
        for c in range(3):
            wall = WROW[pl.ds(CX * c, CX), :]
            pulls.append(double * (U[0, c, pl.ds(1, CX), 0, :] - wall))
        AS[3 + k] = dot(S[...], tall(jnp.concatenate(pulls, axis=0))).reshape(ndev, 8, LANES)
        exchange_start(3 + k)
        exchange_wait(3 + k)
        added = dot(GT[...], AR[3 + k].reshape(8 * ndev, LANES))
        for f in range(6):
            force = load_ref[f]
            if f < 3:
                force = force + added[NB * f : NB * (f + 1)]
            FORCE[f, pl.ds(0, NB), :] = force
            HS[k, 0, pl.ds(f, 1), :] = force[0:1]
            HS[k, 1, pl.ds(f, 1), :] = force[NB - 1 : NB]
            HS[k, 0, pl.ds(8 + f, 1), :] = SH[f, pl.ds(0, 1), :]
            HS[k, 1, pl.ds(8 + f, 1), :] = SH[f, pl.ds(NB - 1, 1), :]
        both("z", lambda side: end_copy(k, side).start())
        both("z", lambda side: end_copy(k, side).wait_send())
        both("z", lambda side: end_copy(k, 1 - side).wait_recv())
        for f in range(6):
            FORCE[f, pl.ds(NB, 8), :] = ends(HR[k, 1, pl.ds(f, 1), :], HR[k, 0, pl.ds(f, 1), :])
            SH[f, pl.ds(NB, 8), :] = ends(HR[k, 1, pl.ds(8 + f, 1), :], HR[k, 0, pl.ds(8 + f, 1), :])
        lax.fori_loop(0, SHELL_SWEEPS, shell_sweep, 0)

        @pl.when(k + 1 < SUBITERS)
        def _():
            send_wall(k + 1)
        return carry

    lax.fori_loop(0, SUBITERS, subiteration, 0)

    for f in range(6):
        sout_ref[f] = SH[f, pl.ds(0, NB), :]

    def give(x, carry):
        for c in range(3):
            for j in range(8):
                uout_ref[c, x, pl.ds(j, 8, stride=8), :] = U[0, c, x + 1, pl.ds(8 * j, 8), :]
        return carry

    lax.fori_loop(0, CX, give, 0)
    for c in range(3):
        both("x", lambda side: u_copy(1, c, side).wait_send())
        both("z", lambda side: z_copy(1, c, side).wait_send())


def body(velocity, source, viscosity, owners, targets, shell_load, shell_state, shell_inverse):
    nsec = lax.axis_size("sec")
    ndev = lax.axis_size("dev")
    owner = owners.reshape(CX)
    place = jnp.arange(CX, dtype=jnp.int32)
    earlier = (owner[:, None] == owner[None, :]) & (place[:, None] < place[None, :])
    rank = jnp.sum(jnp.where(earlier, 1, 0), axis=0).astype(jnp.int32)
    key = owner * 8 + rank
    keys = jnp.concatenate([key, key + 2, key + 4, jnp.full((LANES - ROWS,), -1, jnp.int32)])[None, :]
    name = targets.reshape(CX)
    names = jnp.concatenate([name, name + NB, name + 2 * NB, jnp.full((LANES - ROWS,), -1, jnp.int32)])[None, :]

    vmem = pl.BlockSpec(memory_space=pltpu.VMEM)
    dma = pltpu.SemaphoreType.DMA
    out = pl.pallas_call(
        lambda *refs: kernel(nsec, ndev, *refs),
        out_shape=(
            jax.ShapeDtypeStruct((3, CX, NY, LANES), F32),
            jax.ShapeDtypeStruct((6, NB, LANES), F32),
        ),
        in_specs=[vmem] * 8,
        out_specs=(vmem, vmem),
        scratch_shapes=[
            pltpu.VMEM((2, 3, CX + 2, NY, LANES), F32),
            pltpu.VMEM((CX + 2, NY, LANES), F32),
            pltpu.VMEM((6, CX, NY, LANES), F32),
            pltpu.VMEM((3, CX, NY, LANES), F32),
            pltpu.VMEM((2, 3, 2, 8, LANES), F32),
            pltpu.VMEM((2, 3, 2, 2, 8, LANES), F32),
            pltpu.VMEM((2, 8, LANES), F32),
            pltpu.VMEM((2, 8, LANES), F32),
            pltpu.VMEM((2, 2, 8, LANES), F32),
            pltpu.VMEM((8 * ndev, LANES), F32),
            pltpu.VMEM((LANES, 8 * ndev), F32),
            pltpu.VMEM((8 * ndev, LANES), F32),
            pltpu.VMEM((LANES, 8 * ndev), F32),
            pltpu.VMEM((5, ndev, 8, LANES), F32),
            pltpu.VMEM((5, ndev, 8, LANES), F32),
            pltpu.VMEM((ROWS, LANES), F32),
            pltpu.VMEM((ROWS, 8, LANES), F32),
            pltpu.VMEM((6, 24, LANES), F32),
            pltpu.VMEM((6, 24, LANES), F32),
            pltpu.VMEM((36, 24, LANES), F32),
            pltpu.VMEM((2, 40, LANES), F32),
            pltpu.VMEM((2, 40, LANES), F32),
            pltpu.VMEM((2, 2, 16, LANES), F32),
            pltpu.VMEM((2, 2, 16, LANES), F32),
            dma((2, 3, 2)), dma((2, 3, 2)), dma((2, 3, 2)), dma((2, 3, 2)),
            dma((2,)), dma((2,)), dma((2,)), dma((2,)),
            dma((5,)), dma((5,)),
            dma((2,)), dma((2,)), dma((2, 2)), dma((2, 2)),
        ],
        compiler_params=pltpu.CompilerParams(
            collective_id=0, has_side_effects=True, vmem_limit_bytes=40 * 1024 * 1024),
    )(
        velocity, source, viscosity, keys, names,
        shell_load.reshape(6, NB, LANES), shell_state.reshape(6, NB, LANES),
        shell_inverse.reshape(6, 6, NB, LANES),
    )
    return out[0], out[1].reshape(6, NB * LANES)


def solution(mesh):
    in_specs = (
        P(None, "sec", None, "dev"),
        P(None, "sec", None, "dev"),
        P("sec", None, "dev"),
        P("dev", "sec", None),
        P("dev", "sec"),
        P(None, ("sec", "dev")),
        P(None, ("sec", "dev")),
        P(None, None, ("sec", "dev")),
    )
    out_specs = (P(None, "sec", None, "dev"), P(None, ("sec", "dev")))
    return jax.shard_map(body, mesh=mesh, in_specs=in_specs, out_specs=out_specs, check_vma=False)
```

time: 865 us -> 329 us (0.38)
  Pallas kernels: 0 us -> 317 us
  starting transfers between devices: 230 us -> 0 us
  waiting for transfers between devices: 214 us -> 0 us
  other arithmetic: 202 us -> 2.87 us
  local copies, waits for them, and re-layouts: 160 us -> 7.63 us
  blocking collectives: 47.2 us -> 0 us
    pallas_call x0 -> x1, Pallas kernels: none -> 317 us  [body(): pl.pallas_call(lambda *refs: kernel(nsec, ndev, *refs), out_shape=(jax.Sh...]
    ppermute x100 -> x0, starting transfers between devices: 211 us -> none  [the longest x50 117 us: with_halo(): lax.ppermute(lax.slice_in_dim(block, block.shape[dim] - width, None, axis...]
    ppermute x100 -> x0, waiting for transfers between devices: 205 us -> none  [the longest x50 144 us: with_halo(): lax.ppermute(lax.slice_in_dim(block, block.shape[dim] - width, None, axis...]
    div x16 -> x0, other arithmetic: 176 us -> none  [relax(): return num / denom]
    while x118 -> x0, local copies, waits for them, and re-layouts: 83.6 us -> none
    all_gather x2 -> x0, blocking collectives: 47.2 us -> none  [body(): every = lax.all_gather(blocks, 'dev', axis=0, tiled=True)]
    broadcast_in_dim x16 -> x0, local copies, waits for them, and re-layouts: 46.9 us -> none  [relax(): uy = jnp.concatenate([wall[:, :, None, :], inner, zero_layer], axis=2)]
    slice x54 -> x0, local copies, waits for them, and re-layouts: 19.6 us -> none  [the longest x33 17.5 us: with_halo(): lax.slice_in_dim(block, block.shape[dim] - width, None, axis=dim)]
  transfers between devices with their start and end apart: 103 -> 0, of which waited for: 66 -> 0; matrix products, arithmetic and copies ran while one was open for 21% -> 0% of each run, Pallas kernels for 0% -> 0%
where the time goes in v1:
time: 329 us; the launch traced here: 328 us
  Pallas kernels  317 us (96%)
  local copies, waits for them, and re-layouts  7.63 us (2%)
    pallas_call x1, Pallas kernels, body(): pl.pallas_call(lambda *refs: kernel(nsec, ndev, *refs), out_shape=(jax.Sh...  317 us

profile of v1, /device:TPU:8, one launch (start us, length us, event | category | flops | bytes accessed | tf_op | source)
XLA Modules:
  0.0 328.0 jit_solution(9848998756767723530)
XLA Ops:
  0.6 0.8 select_reduce_fusion
  1.4 0.7 broadcast_add_fusion.3
  2.1 0.7 broadcast_add_fusion.1
  2.8 0.7 fusion.2
  3.5 0.9 copy_bitcast_fusion.1
  4.4 1.1 reshape.28.refs_7_
  5.5 0.0 copy-start
  5.5 1.4 copy-done
  6.9 0.0 copy-start.1
  6.9 1.4 copy-done.1
  8.3 0.0 copy-start.2
  8.3 1.0 copy-done.2
  9.4 316.9 %shard_map.95 = (f32[3,16,64,128]{3,2,1,0:T(8,128)S(1)}, f32[6,16,128]{2,1,0:T(8,128)S(1)}) custom-call(f32[3,16,64,128]{3,2,1,0:T(8,128)S(1)} %copy-done, f32[3,16,64,128]{3,2,1,0:T(8,128)S(1)} %copy-done.1, f32[16,64,128]{2,1,0:T(8,128)S(1)} %copy-done.2, s32[1,128]{1,0:T(1,128)S(1)} %get-tuple-element.9.refs_3_, s32[1,128]{1,0:T(1,128)S(1)} %get-tuple-element.8.refs_4_, ...), custom_call_target="tpu_custom_call" | custom-call | tf_op jit(solution)/shard_map/pallas_call | solution.py:402
  326.3 0.6 copy.16
  326.9 1.1 copy.18
  (1 shorter events, 0.0 us)
Async XLA Ops:
  5.5 1.4 copy-start
  6.9 1.4 copy-start.1
  8.3 1.0 copy-start.2

commit v2 on v1

--- a/solution.py
+++ b/solution.py
@@ -22,7 +22,7 @@
     nsec, ndev,
     vel_ref, src_ref, nu_ref, key_ref, tgt_ref, load_ref, state_ref, inv_ref,
     uout_ref, sout_ref,
-    U, NU, CF, RHS, ZS, ZR, MV, NZS, NZR,
+    UA, UB, NU, CF, RHS, ZS, ZR, NZS, NZR,
     S, ST, G, GT, AS, AR, WROW, WALL,
     SH, FORCE, INV, IS, IR, HS, HR,
     xs_sem, xr_sem, zs_sem, zr_sem, nxs_sem, nxr_sem, nzs_sem, nzr_sem,
@@ -40,8 +40,9 @@
 
     def u_copy(slot, c, side):
         own, there = (CX, 0) if side else (1, CX + 1)
-        return pltpu.make_async_remote_copy(
-            src_ref=U.at[slot, c, own], dst_ref=U.at[slot, c, there],
+        u = (UA, UB)[slot]
+        return pltpu.make_async_remote_copy(
+            src_ref=u.at[c, own], dst_ref=u.at[c, there],
             send_sem=xs_sem.at[slot, c, side], recv_sem=xr_sem.at[slot, c, 1 - side],
             device_id=target("x", side), device_id_type=MESH)
 
@@ -108,33 +109,29 @@
     def tall(rows):
         return jnp.concatenate([rows, jnp.zeros((LANES - ROWS, LANES), F32)], axis=0)
 
-    def pack_plane(ref, x, tiles):
-        packed = tiles[0]
-        for j in range(1, 8):
-            packed = jnp.where((lane == 2 * j) | (lane == 2 * j - 1), pltpu.roll(tiles[j], 2 * j, 1), packed)
-        m = lax.rem(x, 8)
-        packed = pltpu.roll(packed, 16 * m, 1)
-        here = lax.rem(lane + 1, LANES) // 16 == m
-        v = x // 8
-        ref[v] = jnp.where(here, packed, ref[v])
+    def packed(x, tiles, held):
+        for j in range(8):
+            q = 8 * (x % 8) + j
+            here = (lane == 2 * q) | (lane == (2 * q - 1) % LANES)
+            moved = pltpu.roll(tiles[j], 2 * q, 1) if q else tiles[j]
+            held = moved if held is None else jnp.where(here, moved, held)
+        return held
 
     def merged(low, high):
         return jnp.where(lane % 2 == 0, pltpu.roll(low, 1, 1), pltpu.roll(high, LANES - 1, 1))
 
-    def z_pair(tile, mx, j):
-        h = pltpu.roll(mx, (LANES - 2 * j) % LANES, 1)
+    def z_pair(tile, halo, x, j):
+        q = 8 * (x % 8) + j
+        h = pltpu.roll(halo, LANES - 2 * q, 1) if q else halo
         zm = jnp.where(lane == 0, h, pltpu.roll(tile, 1, 1))
         zp = jnp.where(lane == LANES - 1, h, pltpu.roll(tile, LANES - 1, 1))
         return zm, zp
 
-    def halo_row(x):
-        return pltpu.roll(MV[x // 8], lax.rem(LANES - 16 * lax.rem(x, 8), LANES), 1)
-
     zero_plane = jnp.zeros((NY, LANES), F32)
-    for slot in (0, 1):
+    for u in (UA, UB):
         for c in range(3):
-            U[slot, c, 0] = zero_plane
-            U[slot, c, CX + 1] = zero_plane
+            u[c, 0] = zero_plane
+            u[c, CX + 1] = zero_plane
     NU[0] = zero_plane
     NU[CX + 1] = zero_plane
     ZR[...] = jnp.zeros(ZR.shape, F32)
@@ -155,23 +152,32 @@
     lax.fori_loop(1, ndev, greet, 0)
     both("x", lambda side: pl.semaphore_signal(barrier, inc=1, device_id=target("x", side), device_id_type=MESH))
 
-    def take(x, carry):
-        tiles = []
-        for j in range(8):
-            tile = nu_ref[x, pl.ds(j, 8, stride=8), :]
-            NU[x + 1, pl.ds(8 * j, 8), :] = tile
-            tiles.append(tile)
-        pack_plane(NZS, x, tiles)
-        for c in range(3):
-            tiles = []
+    def take(v, carry):
+        held = None
+        for i in range(8):
+            x = 8 * v + i
+            tiles = [nu_ref[x, pl.ds(j, 8, stride=8), :] for j in range(8)]
             for j in range(8):
-                tile = vel_ref[c, x, pl.ds(j, 8, stride=8), :]
-                U[0, c, x + 1, pl.ds(8 * j, 8), :] = tile
-                tiles.append(tile)
-            pack_plane(ZS.at[0, c], x, tiles)
-        return carry
-
-    lax.fori_loop(0, CX, take, 0)
+                NU[x + 1, pl.ds(8 * j, 8), :] = tiles[j]
+            held = packed(i, tiles, held)
+        NZS[v] = held
+        return carry
+
+    lax.fori_loop(0, 2, take, 0)
+
+    def take_velocity(n, carry):
+        c, v = n // 2, lax.rem(n, 2)
+        held = None
+        for i in range(8):
+            x = 8 * v + i
+            tiles = [vel_ref[c, x, pl.ds(j, 8, stride=8), :] for j in range(8)]
+            for j in range(8):
+                UA[c, x + 1, pl.ds(8 * j, 8), :] = tiles[j]
+            held = packed(i, tiles, held)
+        ZS[0, c, v] = held
+        return carry
+
+    lax.fori_loop(0, 6, take_velocity, 0)
     rows256 = lax.broadcasted_iota(jnp.int32, (8 * ndev, LANES), 0)
     one_hot = jnp.where(rows256 == key_ref[...], 1.0, 0.0).astype(F32)
     S[...] = one_hot
@@ -225,30 +231,29 @@
     both("x", lambda side: nu_copy(1 - side).wait_recv())
     both("z", lambda side: nz_copy(side).wait_send())
     both("z", lambda side: nz_copy(1 - side).wait_recv())
-    for v in range(2):
-        MV[v] = merged(NZR[0, v], NZR[1, v])
-
-    def coefficients(x, carry):
-        mx = halo_row(x)
-        tiles = [NU[x + 1, pl.ds(8 * j, 8), :] for j in range(8)]
-        for j in range(8):
-            rows = pl.ds(8 * j, 8)
-            t = tiles[j]
-            zm, zp = z_pair(t, mx, j)
-            ym = tiles[j - 1] if j else jnp.where(sub == 0, t, pltpu.roll(tiles[7], 1, 0))
-            yp = tiles[j + 1] if j < 7 else jnp.where(sub == 7, t, pltpu.roll(tiles[0], 7, 0))
-            faces = [0.5 * (t + o) for o in (NU[x, rows, :], NU[x + 2, rows, :], zm, zp, ym, yp)]
-            total = 1.0 + faces[0]
-            for f in faces[1:]:
-                total = total + f
-            inverse = 1.0 / total
-            for n, f in enumerate(faces):
-                CF[n, x, rows, :] = f * inverse
-            for c in range(3):
-                RHS[c, x, rows, :] = src_ref[c, x, pl.ds(j, 8, stride=8), :] * inverse
-        return carry
-
-    lax.fori_loop(0, CX, coefficients, 0)
+    def coefficients(v, carry):
+        halo = merged(NZR[0, v], NZR[1, v])
+        for i in range(8):
+            x = 8 * v + i
+            tiles = [NU[x + 1, pl.ds(8 * j, 8), :] for j in range(8)]
+            for j in range(8):
+                rows = pl.ds(8 * j, 8)
+                t = tiles[j]
+                zm, zp = z_pair(t, halo, i, j)
+                ym = tiles[j - 1] if j else jnp.where(sub == 0, t, pltpu.roll(tiles[7], 1, 0))
+                yp = tiles[j + 1] if j < 7 else jnp.where(sub == 7, t, pltpu.roll(tiles[0], 7, 0))
+                faces = [0.5 * (t + o) for o in (NU[x, rows, :], NU[x + 2, rows, :], zm, zp, ym, yp)]
+                total = 1.0 + faces[0]
+                for f in faces[1:]:
+                    total = total + f
+                inverse = 1.0 / total
+                for n, f in enumerate(faces):
+                    CF[n, x, rows, :] = f * inverse
+                for c in range(3):
+                    RHS[c, x, rows, :] = src_ref[c, x, pl.ds(j, 8, stride=8), :] * inverse
+        return carry
+
+    lax.fori_loop(0, 2, coefficients, 0)
 
     both("z", lambda side: inv_copy(side).wait_send())
     both("z", lambda side: inv_copy(1 - side).wait_recv())
@@ -258,63 +263,62 @@
             INV[n, pl.ds(0, NB), :] = inv_ref[a, b]
             INV[n, pl.ds(NB, 8), :] = ends(IR[1, pl.ds(n, 1), :], IR[0, pl.ds(n, 1), :])
 
-    def plane(c, x, old, new):
-        mx = halo_row(x)
-        tiles = [U[old, c, x + 1, pl.ds(8 * j, 8), :] for j in range(8)]
+    def plane(c, x, old, new, halo, held):
+        tiles = [old[c, x + 1, pl.ds(8 * j, 8), :] for j in range(8)]
         done = []
         for j in range(8):
             rows = pl.ds(8 * j, 8)
             t = tiles[j]
-            zm, zp = z_pair(t, mx, j)
+            zm, zp = z_pair(t, halo, x, j)
             ym = tiles[j - 1] if j else jnp.where(sub == 0, WALL[c * CX + x], pltpu.roll(tiles[7], 1, 0))
             yp = tiles[j + 1] if j < 7 else jnp.where(sub == 7, 0.0, pltpu.roll(tiles[0], 7, 0))
-            num = RHS[c, x, rows, :] + CF[0, x, rows, :] * U[old, c, x, rows, :]
-            num = num + CF[1, x, rows, :] * U[old, c, x + 2, rows, :]
-            num = num + CF[2, x, rows, :] * zm + CF[3, x, rows, :] * zp
+            num = RHS[c, x, rows, :] + CF[0, x, rows, :] * old[c, x, rows, :]
+            num = num + CF[1, x, rows, :] * old[c, x + 2, rows, :]
             num = num + CF[4, x, rows, :] * ym + CF[5, x, rows, :] * yp
-            U[new, c, x + 1, rows, :] = num
+            num = num + (CF[2, x, rows, :] * zm + CF[3, x, rows, :] * zp)
+            new[c, x + 1, rows, :] = num
             done.append(num)
-        pack_plane(ZS.at[new, c], x, done)
+        return packed(x, done, held)
 
     last = SUBITERS * SWEEPS
 
-    def level(k, carry):
-        new = lax.rem(k, 2)
-        old = 1 - new
+    def level(k, slot):
+        old, new = ((UB, UA), (UA, UB))[slot]
 
         def component(c, carry):
-            both("z", lambda side: z_copy(old, c, 1 - side).wait_recv())
-            for v in range(2):
-                MV[v] = merged(ZR[old, c, 0, v], ZR[old, c, 1, v])
-            both("x", lambda side: u_copy(old, c, 1 - side).wait_recv())
+            both("z", lambda side: z_copy(1 - slot, c, 1 - side).wait_recv())
+            halos = [merged(ZR[1 - slot, c, 0, v], ZR[1 - slot, c, 1, v]) for v in range(2)]
+            both("x", lambda side: u_copy(1 - slot, c, 1 - side).wait_recv())
 
             @pl.when(k >= 2)
             def _():
-                both("x", lambda side: u_copy(new, c, side).wait_send())
-                both("z", lambda side: z_copy(new, c, side).wait_send())
-
-            def edge(i, carry):
-                plane(c, i * (CX - 1), old, new)
-                return carry
-
-            lax.fori_loop(0, 2, edge, 0)
+                both("x", lambda side: u_copy(slot, c, side).wait_send())
+                both("z", lambda side: z_copy(slot, c, side).wait_send())
+
+            first = plane(c, 0, old, new, halos[0], None)
+            second = plane(c, CX - 1, old, new, halos[1], None)
 
             @pl.when(k < last)
             def _():
-                both("x", lambda side: u_copy(new, c, side).start())
-
-            def inner(x, carry):
-                plane(c, x, old, new)
-                return carry
-
-            lax.fori_loop(1, CX - 1, inner, 0)
+                both("x", lambda side: u_copy(slot, c, side).start())
+
+            for x in range(1, CX // 2):
+                first = plane(c, x, old, new, halos[0], first)
+            ZS[slot, c, 0] = first
+            for x in range(CX // 2, CX - 1):
+                second = plane(c, x, old, new, halos[1], second)
+            ZS[slot, c, 1] = second
 
             @pl.when(k < last)
             def _():
-                both("z", lambda side: z_copy(new, c, side).start())
+                both("z", lambda side: z_copy(slot, c, side).start())
             return carry
 
         lax.fori_loop(0, 3, component, 0)
+
+    def levels(n, carry):
+        level(2 * n + 1, 1)
+        level(2 * n + 2, 0)
         return carry
 
     def shell_sweep(step, carry):
@@ -336,12 +340,12 @@
 
     def subiteration(k, carry):
         take_wall(k)
-        lax.fori_loop(k * SWEEPS + 1, (k + 1) * SWEEPS + 1, level, 0)
+        lax.fori_loop(k * (SWEEPS // 2), (k + 1) * (SWEEPS // 2), levels, 0)
         double = 2.0 * NU[pl.ds(1, CX), 0, :]
         pulls = []
         for c in range(3):
             wall = WROW[pl.ds(CX * c, CX), :]
-            pulls.append(double * (U[0, c, pl.ds(1, CX), 0, :] - wall))
+            pulls.append(double * (UA[c, pl.ds(1, CX), 0, :] - wall))
         AS[3 + k] = dot(S[...], tall(jnp.concatenate(pulls, axis=0))).reshape(ndev, 8, LANES)
         exchange_start(3 + k)
         exchange_wait(3 + k)
@@ -376,7 +380,7 @@
     def give(x, carry):
         for c in range(3):
             for j in range(8):
-                uout_ref[c, x, pl.ds(j, 8, stride=8), :] = U[0, c, x + 1, pl.ds(8 * j, 8), :]
+                uout_ref[c, x, pl.ds(j, 8, stride=8), :] = UA[c, x + 1, pl.ds(8 * j, 8), :]
         return carry
 
     lax.fori_loop(0, CX, give, 0)
@@ -408,13 +412,13 @@
         in_specs=[vmem] * 8,
         out_specs=(vmem, vmem),
         scratch_shapes=[
-            pltpu.VMEM((2, 3, CX + 2, NY, LANES), F32),
+            pltpu.VMEM((3, CX + 2, NY, LANES), F32),
+            pltpu.VMEM((3, CX + 2, NY, LANES), F32),
             pltpu.VMEM((CX + 2, NY, LANES), F32),
             pltpu.VMEM((6, CX, NY, LANES), F32),
             pltpu.VMEM((3, CX, NY, LANES), F32),
             pltpu.VMEM((2, 3, 2, 8, LANES), F32),
             pltpu.VMEM((2, 3, 2, 2, 8, LANES), F32),
-            pltpu.VMEM((2, 8, LANES), F32),
             pltpu.VMEM((2, 8, LANES), F32),
             pltpu.VMEM((2, 2, 8, LANES), F32),
             pltpu.VMEM((8 * ndev, LANES), F32),

time: 329 us -> 126 us (0.38)
  Pallas kernels: 317 us -> 114 us
    pallas_call x1, Pallas kernels: 317 us -> 114 us  [body(): pl.pallas_call(lambda *refs: kernel(nsec, ndev, *refs), out_shape=(jax.Sh...]
where the time goes in v2:
time: 126 us
  Pallas kernels  114 us (90%)
  local copies, waits for them, and re-layouts  7.63 us (6%)
  other arithmetic  2.87 us (2%)
    pallas_call x1, Pallas kernels, body(): pl.pallas_call(lambda *refs: kernel(nsec, ndev, *refs), out_shape=(jax.Sh...  114 us
    unnamed x8, local copies, waits for them, and re-layouts  5.64 us

profile of v2, /device:TPU:8, one launch (start us, length us, event | category | flops | bytes accessed | tf_op | source)
XLA Modules:
  0.0 125.6 jit_solution(16732154722940256481)
XLA Ops:
  0.6 0.8 select_reduce_fusion
  1.4 0.7 broadcast_add_fusion.3
  2.1 0.7 broadcast_add_fusion.1
  2.8 0.7 fusion.2
  3.5 0.9 copy_bitcast_fusion.1
  4.4 1.1 reshape.28.refs_7_
  5.5 0.0 copy-start
  5.5 1.4 %copy-done = f32[3,16,64,128]{3,2,1,0:T(8,128)S(1)} copy-done((f32[3,16,64,128]{3,2,1,0:T(8,128)S(1)}, f32[3,16,64,128]{3,2,1,0:T(8,128)}, u32[]{:S(2)}) %copy-start) | copy-done | bytes 1572888
  6.9 0.0 copy-start.1
  6.9 1.4 %copy-done.1 = f32[3,16,64,128]{3,2,1,0:T(8,128)S(1)} copy-done((f32[3,16,64,128]{3,2,1,0:T(8,128)S(1)}, f32[3,16,64,128]{3,2,1,0:T(8,128)}, u32[]{:S(2)}) %copy-start.1) | copy-done | bytes 1572888
  8.3 0.0 copy-start.2
  8.3 1.0 copy-done.2
  9.4 114.5 %shard_map.95 = (f32[3,16,64,128]{3,2,1,0:T(8,128)S(1)}, f32[6,16,128]{2,1,0:T(8,128)S(1)}) custom-call(f32[3,16,64,128]{3,2,1,0:T(8,128)S(1)} %copy-done, f32[3,16,64,128]{3,2,1,0:T(8,128)S(1)} %copy-done.1, f32[16,64,128]{2,1,0:T(8,128)S(1)} %copy-done.2, s32[1,128]{1,0:T(1,128)S(1)} %get-tuple-element.9.refs_3_, s32[1,128]{1,0:T(1,128)S(1)} %get-tuple-element.8.refs_4_, ...), custom_call_target="tpu_custom_call" | custom-call | tf_op jit(solution)/shard_map/pallas_call | solution.py:406
  123.8 0.6 copy.16
  124.5 1.1 copy.18
  (1 shorter events, 0.0 us)
Async XLA Ops:
  5.5 1.4 %copy-start = (f32[3,16,64,128]{3,2,1,0:T(8,128)S(1)}, f32[3,16,64,128]{3,2,1,0:T(8,128)}, u32[]{:S(2)}) copy-start(f32[3,16,64,128]{3,2,1,0:T(8,128)} %refs_0_.1) | copy-start | bytes 4718596
  6.9 1.4 %copy-start.1 = (f32[3,16,64,128]{3,2,1,0:T(8,128)S(1)}, f32[3,16,64,128]{3,2,1,0:T(8,128)}, u32[]{:S(2)}) copy-start(f32[3,16,64,128]{3,2,1,0:T(8,128)} %refs_1_.1) | copy-start | bytes 4718596
  8.3 1.0 copy-start.2

commit v3 on v2

--- a/solution.py
+++ b/solution.py
@@ -22,8 +22,8 @@
     nsec, ndev,
     vel_ref, src_ref, nu_ref, key_ref, tgt_ref, load_ref, state_ref, inv_ref,
     uout_ref, sout_ref,
-    UA, UB, NU, CF, RHS, ZS, ZR, NZS, NZR,
-    S, ST, G, GT, AS, AR, WROW, WALL,
+    UA, UB, NU, CF, CW, RHS, RW, ZS, ZR, NZS, NZR,
+    S, ST, G, GT, AS, AR, WT, PULL, N2,
     SH, FORCE, INV, IS, IR, HS, HR,
     xs_sem, xr_sem, zs_sem, zr_sem, nxs_sem, nxr_sem, nzs_sem, nzr_sem,
     as_sem, ar_sem, is_sem, ir_sem, hs_sem, hr_sem,
@@ -55,7 +55,7 @@
     def nu_copy(side):
         own, there = (CX, 0) if side else (1, CX + 1)
         return pltpu.make_async_remote_copy(
-            src_ref=NU.at[own], dst_ref=NU.at[there],
+            src_ref=NU.at[0, own], dst_ref=NU.at[0, there],
             send_sem=nxs_sem.at[side], recv_sem=nxr_sem.at[1 - side],
             device_id=target("x", side), device_id_type=MESH)
 
@@ -109,31 +109,40 @@
     def tall(rows):
         return jnp.concatenate([rows, jnp.zeros((LANES - ROWS, LANES), F32)], axis=0)
 
-    def packed(x, tiles, held):
-        for j in range(8):
-            q = 8 * (x % 8) + j
-            here = (lane == 2 * q) | (lane == (2 * q - 1) % LANES)
-            moved = pltpu.roll(tiles[j], 2 * q, 1) if q else tiles[j]
-            held = moved if held is None else jnp.where(here, moved, held)
-        return held
-
-    def merged(low, high):
-        return jnp.where(lane % 2 == 0, pltpu.roll(low, 1, 1), pltpu.roll(high, LANES - 1, 1))
-
-    def z_pair(tile, halo, x, j):
-        q = 8 * (x % 8) + j
-        h = pltpu.roll(halo, LANES - 2 * q, 1) if q else halo
-        zm = jnp.where(lane == 0, h, pltpu.roll(tile, 1, 1))
-        zp = jnp.where(lane == LANES - 1, h, pltpu.roll(tile, LANES - 1, 1))
+    half = lane < LANES // 2
+    half16 = lax.broadcasted_iota(jnp.int32, (CX, LANES), 1) < LANES // 2
+
+    def turn(first, second):
+        top = [jnp.where(half, first[n], pltpu.roll(second[n], LANES // 2, 1)) for n in range(8)]
+        low = [jnp.where(half, pltpu.roll(first[n], LANES // 2, 1), second[n]) for n in range(8)]
+        return jnp.concatenate(top + low, axis=0).T
+
+    def spread(ref, c, x, rows):
+        for m in range(8):
+            ref[c, x, pl.ds(m, 8, stride=8), :] = rows[8 * m : 8 * m + 8]
+
+    def face_rows(low, high):
+        return jnp.where(half16, low, high)
+
+    def beside(low, high, before, after):
+        inner = pltpu.roll(jnp.where(half16, high, low), LANES // 2, 1)
+        zm = jnp.where(half16, pltpu.roll(before, LANES // 2, 1), inner)
+        zp = jnp.where(half16, inner, pltpu.roll(after, LANES // 2, 1))
         return zm, zp
+
+    def z_first(row, tile):
+        return jnp.where(sub == 0, row, pltpu.roll(tile, 1, 0))
+
+    def z_last(row, tile):
+        return jnp.where(sub == 7, row, pltpu.roll(tile, 7, 0))
 
     zero_plane = jnp.zeros((NY, LANES), F32)
     for u in (UA, UB):
         for c in range(3):
             u[c, 0] = zero_plane
             u[c, CX + 1] = zero_plane
-    NU[0] = zero_plane
-    NU[CX + 1] = zero_plane
+    NU[0, 0] = zero_plane
+    NU[0, CX + 1] = zero_plane
     ZR[...] = jnp.zeros(ZR.shape, F32)
     ZS[...] = jnp.zeros(ZS.shape, F32)
     NZR[...] = jnp.zeros(NZR.shape, F32)
@@ -152,32 +161,24 @@
     lax.fori_loop(1, ndev, greet, 0)
     both("x", lambda side: pl.semaphore_signal(barrier, inc=1, device_id=target("x", side), device_id_type=MESH))
 
-    def take(v, carry):
-        held = None
-        for i in range(8):
-            x = 8 * v + i
-            tiles = [nu_ref[x, pl.ds(j, 8, stride=8), :] for j in range(8)]
-            for j in range(8):
-                NU[x + 1, pl.ds(8 * j, 8), :] = tiles[j]
-            held = packed(i, tiles, held)
-        NZS[v] = held
-        return carry
-
-    lax.fori_loop(0, 2, take, 0)
-
-    def take_velocity(n, carry):
-        c, v = n // 2, lax.rem(n, 2)
-        held = None
-        for i in range(8):
-            x = 8 * v + i
-            tiles = [vel_ref[c, x, pl.ds(j, 8, stride=8), :] for j in range(8)]
-            for j in range(8):
-                UA[c, x + 1, pl.ds(8 * j, 8), :] = tiles[j]
-            held = packed(i, tiles, held)
-        ZS[0, c, v] = held
-        return carry
-
-    lax.fori_loop(0, 6, take_velocity, 0)
+    def take(refs):
+        def step(i, carry):
+            for ref, c, out, d, shift in refs:
+                first = [ref[c, 2 * i, pl.ds(8 * n, 8), :] for n in range(8)]
+                second = [ref[c, 2 * i + 1, pl.ds(8 * n, 8), :] for n in range(8)]
+                rows = turn(first, second)
+                spread(out, d, 2 * i + shift, rows[:NY])
+                spread(out, d, 2 * i + 1 + shift, rows[NY:])
+            return carry
+
+        lax.fori_loop(0, CX // 2, step, 0)
+
+    take([(nu_ref, 0, NU, 0, 1)] + [(vel_ref, c, UA, c, 1) for c in range(3)])
+    NZS[...] = face_rows(NU[0, pl.ds(1, CX), 0, :], NU[0, pl.ds(1, CX), NY - 1, :])
+    for c in range(3):
+        ZS[0, c] = face_rows(UA[c, pl.ds(1, CX), 0, :], UA[c, pl.ds(1, CX), NY - 1, :])
+    wet = nu_ref[0, :, 0, :]
+    N2[...] = 2.0 * tall(jnp.concatenate([wet, wet, wet], axis=0)).T
     rows256 = lax.broadcasted_iota(jnp.int32, (8 * ndev, LANES), 0)
     one_hot = jnp.where(rows256 == key_ref[...], 1.0, 0.0).astype(F32)
     S[...] = one_hot
@@ -221,39 +222,53 @@
     def take_wall(k):
         exchange_wait(1 + k)
         wall = dot(ST[...], AR[1 + k].reshape(8 * ndev, LANES))
-        WROW[...] = wall[:ROWS]
+        WT[...] = wall.T
+        tiles = [
+            jnp.where(
+                half,
+                WT[pl.ds(j, 8, stride=8), :],
+                pltpu.roll(WT[pl.ds(NY + j, 8, stride=8), :], LANES // 2, 1))
+            for j in range(8)
+        ]
         for q in range(ROWS):
-            WALL[q] = jnp.broadcast_to(wall[q : q + 1], (8, LANES))
+            c, x = q // CX, q % CX
+            for j in range(8):
+                rows = pl.ds(8 * j, 8)
+                wall = pltpu.roll(tiles[j], LANES - q, 1) if q else tiles[j]
+                RW[c, x, rows, :] = RHS[c, x, rows, :] + CW[x, rows, :] * wall
 
     send_wall(0)
+    take([(src_ref, c, RHS, c, 0) for c in range(3)])
 
     both("x", lambda side: nu_copy(side).wait_send())
     both("x", lambda side: nu_copy(1 - side).wait_recv())
     both("z", lambda side: nz_copy(side).wait_send())
     both("z", lambda side: nz_copy(1 - side).wait_recv())
-    def coefficients(v, carry):
-        halo = merged(NZR[0, v], NZR[1, v])
-        for i in range(8):
-            x = 8 * v + i
-            tiles = [NU[x + 1, pl.ds(8 * j, 8), :] for j in range(8)]
-            for j in range(8):
-                rows = pl.ds(8 * j, 8)
-                t = tiles[j]
-                zm, zp = z_pair(t, halo, i, j)
-                ym = tiles[j - 1] if j else jnp.where(sub == 0, t, pltpu.roll(tiles[7], 1, 0))
-                yp = tiles[j + 1] if j < 7 else jnp.where(sub == 7, t, pltpu.roll(tiles[0], 7, 0))
-                faces = [0.5 * (t + o) for o in (NU[x, rows, :], NU[x + 2, rows, :], zm, zp, ym, yp)]
-                total = 1.0 + faces[0]
-                for f in faces[1:]:
-                    total = total + f
-                inverse = 1.0 / total
-                for n, f in enumerate(faces):
-                    CF[n, x, rows, :] = f * inverse
-                for c in range(3):
-                    RHS[c, x, rows, :] = src_ref[c, x, pl.ds(j, 8, stride=8), :] * inverse
-        return carry
-
-    lax.fori_loop(0, 2, coefficients, 0)
+    nzm, nzp = beside(NU[0, pl.ds(1, CX), 0, :], NU[0, pl.ds(1, CX), NY - 1, :], NZR[0], NZR[1])
+    y_first = lane % NY == 0
+    y_last = lane % NY == NY - 1
+    for x in range(CX):
+        tiles = [NU[0, x + 1, pl.ds(8 * j, 8), :] for j in range(8)]
+        for j in range(8):
+            rows = pl.ds(8 * j, 8)
+            t = tiles[j]
+            zm = tiles[j - 1] if j else z_first(nzm[x : x + 1], tiles[7])
+            zp = tiles[j + 1] if j < 7 else z_last(nzp[x : x + 1], tiles[0])
+            ym = jnp.where(y_first, t, pltpu.roll(t, 1, 1))
+            yp = jnp.where(y_last, t, pltpu.roll(t, LANES - 1, 1))
+            faces = [0.5 * (t + o) for o in (NU[0, x, rows, :], NU[0, x + 2, rows, :], zm, zp, ym, yp)]
+            total = 1.0 + faces[0]
+            for f in faces[1:]:
+                total = total + f
+            inverse = 1.0 / total
+            for n in range(4):
+                CF[n, x, rows, :] = faces[n] * inverse
+            below = faces[4] * inverse
+            CW[x, rows, :] = jnp.where(y_first, below, 0.0)
+            CF[4, x, rows, :] = jnp.where(y_first, 0.0, below)
+            CF[5, x, rows, :] = jnp.where(y_last, 0.0, faces[5] * inverse)
+            for c in range(3):
+                RHS[c, x, rows, :] = RHS[c, x, rows, :] * inverse
 
     both("z", lambda side: inv_copy(side).wait_send())
     both("z", lambda side: inv_copy(1 - side).wait_recv())
@@ -263,22 +278,18 @@
             INV[n, pl.ds(0, NB), :] = inv_ref[a, b]
             INV[n, pl.ds(NB, 8), :] = ends(IR[1, pl.ds(n, 1), :], IR[0, pl.ds(n, 1), :])
 
-    def plane(c, x, old, new, halo, held):
+    def plane(c, x, old, new, zms, zps):
         tiles = [old[c, x + 1, pl.ds(8 * j, 8), :] for j in range(8)]
-        done = []
         for j in range(8):
             rows = pl.ds(8 * j, 8)
             t = tiles[j]
-            zm, zp = z_pair(t, halo, x, j)
-            ym = tiles[j - 1] if j else jnp.where(sub == 0, WALL[c * CX + x], pltpu.roll(tiles[7], 1, 0))
-            yp = tiles[j + 1] if j < 7 else jnp.where(sub == 7, 0.0, pltpu.roll(tiles[0], 7, 0))
-            num = RHS[c, x, rows, :] + CF[0, x, rows, :] * old[c, x, rows, :]
+            zm = tiles[j - 1] if j else z_first(zms[x : x + 1], tiles[7])
+            zp = tiles[j + 1] if j < 7 else z_last(zps[x : x + 1], tiles[0])
+            num = RW[c, x, rows, :] + CF[0, x, rows, :] * old[c, x, rows, :]
             num = num + CF[1, x, rows, :] * old[c, x + 2, rows, :]
-            num = num + CF[4, x, rows, :] * ym + CF[5, x, rows, :] * yp
-            num = num + (CF[2, x, rows, :] * zm + CF[3, x, rows, :] * zp)
-            new[c, x + 1, rows, :] = num
-            done.append(num)
-        return packed(x, done, held)
+            num = num + CF[2, x, rows, :] * zm + CF[3, x, rows, :] * zp
+            ys = CF[4, x, rows, :] * pltpu.roll(t, 1, 1) + CF[5, x, rows, :] * pltpu.roll(t, LANES - 1, 1)
+            new[c, x + 1, rows, :] = num + ys
 
     last = SUBITERS * SWEEPS
 
@@ -287,7 +298,9 @@
 
         def component(c, carry):
             both("z", lambda side: z_copy(1 - slot, c, 1 - side).wait_recv())
-            halos = [merged(ZR[1 - slot, c, 0, v], ZR[1 - slot, c, 1, v]) for v in range(2)]
+            zms, zps = beside(
+                old[c, pl.ds(1, CX), 0, :], old[c, pl.ds(1, CX), NY - 1, :],
+                ZR[1 - slot, c, 0], ZR[1 - slot, c, 1])
             both("x", lambda side: u_copy(1 - slot, c, 1 - side).wait_recv())
 
             @pl.when(k >= 2)
@@ -295,19 +308,16 @@
                 both("x", lambda side: u_copy(slot, c, side).wait_send())
                 both("z", lambda side: z_copy(slot, c, side).wait_send())
 
-            first = plane(c, 0, old, new, halos[0], None)
-            second = plane(c, CX - 1, old, new, halos[1], None)
+            plane(c, 0, old, new, zms, zps)
+            plane(c, CX - 1, old, new, zms, zps)
 
             @pl.when(k < last)
             def _():
                 both("x", lambda side: u_copy(slot, c, side).start())
 
-            for x in range(1, CX // 2):
-                first = plane(c, x, old, new, halos[0], first)
-            ZS[slot, c, 0] = first
-            for x in range(CX // 2, CX - 1):
-                second = plane(c, x, old, new, halos[1], second)
-            ZS[slot, c, 1] = second
+            for x in range(1, CX - 1):
+                plane(c, x, old, new, zms, zps)
+            ZS[slot, c] = face_rows(new[c, pl.ds(1, CX), 0, :], new[c, pl.ds(1, CX), NY - 1, :])
 
             @pl.when(k < last)
             def _():
@@ -341,12 +351,17 @@
     def subiteration(k, carry):
         take_wall(k)
         lax.fori_loop(k * (SWEEPS // 2), (k + 1) * (SWEEPS // 2), levels, 0)
-        double = 2.0 * NU[pl.ds(1, CX), 0, :]
-        pulls = []
-        for c in range(3):
-            wall = WROW[pl.ds(CX * c, CX), :]
-            pulls.append(double * (UA[c, pl.ds(1, CX), 0, :] - wall))
-        AS[3 + k] = dot(S[...], tall(jnp.concatenate(pulls, axis=0))).reshape(ndev, 8, LANES)
+        tiles = [jnp.zeros((8, LANES), F32) for j in range(8)]
+        for q in range(ROWS):
+            here = (lane == q) | (lane == q + NY)
+            for j in range(8):
+                tile = UA[q // CX, q % CX + 1, pl.ds(8 * j, 8), :]
+                tiles[j] = jnp.where(here, pltpu.roll(tile, q, 1) if q else tile, tiles[j])
+        for j in range(8):
+            PULL[pl.ds(j, 8, stride=8), :] = jnp.where(half, tiles[j], 0.0)
+            PULL[pl.ds(NY + j, 8, stride=8), :] = jnp.where(half, pltpu.roll(tiles[j], LANES // 2, 1), 0.0)
+        pulls = N2[...] * (PULL[...] - WT[...])
+        AS[3 + k] = dot(S[...], pulls.T).reshape(ndev, 8, LANES)
         exchange_start(3 + k)
         exchange_wait(3 + k)
         added = dot(GT[...], AR[3 + k].reshape(8 * ndev, LANES))
@@ -377,13 +392,17 @@
     for f in range(6):
         sout_ref[f] = SH[f, pl.ds(0, NB), :]
 
-    def give(x, carry):
+    def give(i, carry):
         for c in range(3):
-            for j in range(8):
-                uout_ref[c, x, pl.ds(j, 8, stride=8), :] = UA[c, x + 1, pl.ds(8 * j, 8), :]
+            rows = jnp.concatenate(
+                [UA[c, 2 * i + 1 + p, pl.ds(m, 8, stride=8), :] for p in range(2) for m in range(8)], axis=0).T
+            for n in range(8):
+                top, low = rows[8 * n : 8 * n + 8], rows[NY + 8 * n : NY + 8 * n + 8]
+                uout_ref[c, 2 * i, pl.ds(8 * n, 8), :] = jnp.where(half, top, pltpu.roll(low, LANES // 2, 1))
+                uout_ref[c, 2 * i + 1, pl.ds(8 * n, 8), :] = jnp.where(half, pltpu.roll(top, LANES // 2, 1), low)
         return carry
 
-    lax.fori_loop(0, CX, give, 0)
+    lax.fori_loop(0, CX // 2, give, 0)
     for c in range(3):
         both("x", lambda side: u_copy(1, c, side).wait_send())
         both("z", lambda side: z_copy(1, c, side).wait_send())
@@ -414,21 +433,24 @@
         scratch_shapes=[
             pltpu.VMEM((3, CX + 2, NY, LANES), F32),
             pltpu.VMEM((3, CX + 2, NY, LANES), F32),
-            pltpu.VMEM((CX + 2, NY, LANES), F32),
+            pltpu.VMEM((1, CX + 2, NY, LANES), F32),
             pltpu.VMEM((6, CX, NY, LANES), F32),
+            pltpu.VMEM((CX, NY, LANES), F32),
             pltpu.VMEM((3, CX, NY, LANES), F32),
-            pltpu.VMEM((2, 3, 2, 8, LANES), F32),
-            pltpu.VMEM((2, 3, 2, 2, 8, LANES), F32),
-            pltpu.VMEM((2, 8, LANES), F32),
-            pltpu.VMEM((2, 2, 8, LANES), F32),
+            pltpu.VMEM((3, CX, NY, LANES), F32),
+            pltpu.VMEM((2, 3, CX, LANES), F32),
+            pltpu.VMEM((2, 3, 2, CX, LANES), F32),
+            pltpu.VMEM((CX, LANES), F32),
+            pltpu.VMEM((2, CX, LANES), F32),
             pltpu.VMEM((8 * ndev, LANES), F32),
             pltpu.VMEM((LANES, 8 * ndev), F32),
             pltpu.VMEM((8 * ndev, LANES), F32),
             pltpu.VMEM((LANES, 8 * ndev), F32),
             pltpu.VMEM((5, ndev, 8, LANES), F32),
             pltpu.VMEM((5, ndev, 8, LANES), F32),
-            pltpu.VMEM((ROWS, LANES), F32),
-            pltpu.VMEM((ROWS, 8, LANES), F32),
+            pltpu.VMEM((LANES, LANES), F32),
+            pltpu.VMEM((LANES, LANES), F32),
+            pltpu.VMEM((LANES, LANES), F32),
             pltpu.VMEM((6, 24, LANES), F32),
             pltpu.VMEM((6, 24, LANES), F32),
             pltpu.VMEM((36, 24, LANES), F32),
@@ -444,7 +466,7 @@
         compiler_params=pltpu.CompilerParams(
             collective_id=0, has_side_effects=True, vmem_limit_bytes=40 * 1024 * 1024),
     )(
-        velocity, source, viscosity, keys, names,
+        velocity, source, viscosity[None], keys, names,
         shell_load.reshape(6, NB, LANES), shell_state.reshape(6, NB, LANES),
         shell_inverse.reshape(6, 6, NB, LANES),
     )

time: 126 us -> 114 us (0.905)
  Pallas kernels: 114 us -> 103 us
    pallas_call x1, Pallas kernels: 114 us -> 103 us  [body(): pl.pallas_call(lambda *refs: kernel(nsec, ndev, *refs), out_shape=(jax.Sh...]
where the time goes in v3:
time: 114 us
  Pallas kernels  103 us (90%)
  local copies, waits for them, and re-layouts  7.63 us (7%)
  other arithmetic  2.87 us (3%)
    pallas_call x1, Pallas kernels, body(): pl.pallas_call(lambda *refs: kernel(nsec, ndev, *refs), out_shape=(jax.Sh...  103 us
    unnamed x8, local copies, waits for them, and re-layouts  5.64 us

profile of v3, /device:TPU:8, one launch (start us, length us, event | category | flops | bytes accessed | tf_op | source)
XLA Modules:
  0.0 113.7 jit_solution(1340363423415930556)
XLA Ops:
  0.6 0.8 select_reduce_fusion
  1.4 0.7 broadcast_add_fusion.3
  2.1 0.7 broadcast_add_fusion.1
  2.8 0.7 fusion.2
  3.5 0.9 copy_bitcast_fusion.1
  4.4 1.1 reshape.28.refs_7_
  5.5 0.0 copy-start
  5.5 1.4 %copy-done = f32[3,16,64,128]{3,2,1,0:T(8,128)S(1)} copy-done((f32[3,16,64,128]{3,2,1,0:T(8,128)S(1)}, f32[3,16,64,128]{3,2,1,0:T(8,128)}, u32[]{:S(2)}) %copy-start) | copy-done | bytes 1572888
  6.9 0.0 copy-start.1
  6.9 1.4 %copy-done.1 = f32[3,16,64,128]{3,2,1,0:T(8,128)S(1)} copy-done((f32[3,16,64,128]{3,2,1,0:T(8,128)S(1)}, f32[3,16,64,128]{3,2,1,0:T(8,128)}, u32[]{:S(2)}) %copy-start.1) | copy-done | bytes 1572888
  8.3 0.0 copy-start.2
  8.3 1.0 copy-done.2
  9.4 102.5 %shard_map.95 = (f32[3,16,64,128]{3,2,1,0:T(8,128)S(1)}, f32[6,16,128]{2,1,0:T(8,128)S(1)}) custom-call(f32[3,16,64,128]{3,2,1,0:T(8,128)S(1)} %copy-done, f32[3,16,64,128]{3,2,1,0:T(8,128)S(1)} %copy-done.1, f32[1,16,64,128]{3,2,1,0:T(8,128)S(1)} %bitcast.21, s32[1,128]{1,0:T(1,128)S(1)} %get-tuple-element.9.refs_3_, ...), custom_call_target="tpu_custom_call" | custom-call | tf_op jit(solution)/shard_map/pallas_call | solution.py:425
  111.9 0.6 copy.16
  112.5 1.1 %copy.18 = f32[3,16,64,128]{3,2,1,0:T(8,128)} copy(f32[3,16,64,128]{3,2,1,0:T(8,128)S(1)} %get-tuple-element.17) | data formatting | bytes 3145728
  (1 shorter events, 0.0 us)
Async XLA Ops:
  5.5 1.4 %copy-start = (f32[3,16,64,128]{3,2,1,0:T(8,128)S(1)}, f32[3,16,64,128]{3,2,1,0:T(8,128)}, u32[]{:S(2)}) copy-start(f32[3,16,64,128]{3,2,1,0:T(8,128)} %refs_0_.1) | copy-start | bytes 4718596
  6.9 1.4 %copy-start.1 = (f32[3,16,64,128]{3,2,1,0:T(8,128)S(1)}, f32[3,16,64,128]{3,2,1,0:T(8,128)}, u32[]{:S(2)}) copy-start(f32[3,16,64,128]{3,2,1,0:T(8,128)} %refs_1_.1) | copy-start | bytes 4718596
  8.3 1.0 copy-start.2

commit v4 on v3

--- a/solution.py
+++ b/solution.py
@@ -22,10 +22,13 @@
     nsec, ndev,
     vel_ref, src_ref, nu_ref, key_ref, tgt_ref, load_ref, state_ref, inv_ref,
     uout_ref, sout_ref,
-    UA, UB, NU, CF, CW, RHS, RW, ZS, ZR, NZS, NZR,
-    S, ST, G, GT, AS, AR, WT, PULL, N2,
+    UA, UB, NU, CF, CW, SRC, RHS, RW, XR, ZS, ZR, CS, CR,
+    NXR, NZS, NZR, NCS, NCR, SXR, EC, ECR, HC, RH,
+    S, ST, G, GT, AS, AR, WT, WQ, WX, WXR, WZR, PULL, N2,
     SH, FORCE, INV, IS, IR, HS, HR,
-    xs_sem, xr_sem, zs_sem, zr_sem, nxs_sem, nxr_sem, nzs_sem, nzr_sem,
+    xs_sem, xr_sem, zs_sem, zr_sem, cs_sem, cr_sem,
+    nxs_sem, nxr_sem, nzs_sem, nzr_sem, ncs_sem, ncr_sem, ss_sem, sr_sem, es_sem, er_sem,
+    wxs_sem, wxr_sem, wzs_sem, wzr_sem,
     as_sem, ar_sem, is_sem, ir_sem, hs_sem, hr_sem,
 ):
     sec = lax.axis_index("sec")
@@ -38,32 +41,51 @@
         step = 1 if side else -1
         return {"sec": sec + step} if axis == "x" else {"dev": dev + step}
 
-    def u_copy(slot, c, side):
-        own, there = (CX, 0) if side else (1, CX + 1)
-        u = (UA, UB)[slot]
+    def remote(src, dst, send_sem, recv_sem, device):
         return pltpu.make_async_remote_copy(
-            src_ref=u.at[c, own], dst_ref=u.at[c, there],
-            send_sem=xs_sem.at[slot, c, side], recv_sem=xr_sem.at[slot, c, 1 - side],
-            device_id=target("x", side), device_id_type=MESH)
-
-    def z_copy(slot, c, side):
-        return pltpu.make_async_remote_copy(
-            src_ref=ZS.at[slot, c], dst_ref=ZR.at[slot, c, 1 - side],
-            send_sem=zs_sem.at[slot, c, side], recv_sem=zr_sem.at[slot, c, 1 - side],
-            device_id=target("z", side), device_id_type=MESH)
+            src_ref=src, dst_ref=dst, send_sem=send_sem, recv_sem=recv_sem,
+            device_id=device, device_id_type=MESH)
+
+    def u_copy(p, c, side):
+        return remote(UA.at[c, pl.ds((CX - 2) * side, 2)], XR.at[p, c, 1 - side],
+                      xs_sem.at[p, c, side], xr_sem.at[p, c, 1 - side], target("x", side))
+
+    def z_copy(p, c, side):
+        return remote(ZS.at[p, c], ZR.at[p, c, 1 - side],
+                      zs_sem.at[p, c, side], zr_sem.at[p, c, 1 - side], target("z", side))
+
+    def corner(a, b):
+        return {"sec": sec + 2 * a - 1, "dev": dev + 2 * b - 1}
+
+    def c_copy(p, c, a, b):
+        return remote(CS.at[p, c, a], CR.at[p, c, 1 - a, 1 - b],
+                      cs_sem.at[p, c, a, b], cr_sem.at[p, c, 1 - a, 1 - b], corner(a, b))
 
     def nu_copy(side):
-        own, there = (CX, 0) if side else (1, CX + 1)
-        return pltpu.make_async_remote_copy(
-            src_ref=NU.at[0, own], dst_ref=NU.at[0, there],
-            send_sem=nxs_sem.at[side], recv_sem=nxr_sem.at[1 - side],
-            device_id=target("x", side), device_id_type=MESH)
+        return remote(NU.at[0, pl.ds((CX - 2) * side, 2)], NXR.at[1 - side],
+                      nxs_sem.at[side], nxr_sem.at[1 - side], target("x", side))
 
     def nz_copy(side):
-        return pltpu.make_async_remote_copy(
-            src_ref=NZS, dst_ref=NZR.at[1 - side],
-            send_sem=nzs_sem.at[side], recv_sem=nzr_sem.at[1 - side],
-            device_id=target("z", side), device_id_type=MESH)
+        return remote(NZS, NZR.at[1 - side], nzs_sem.at[side], nzr_sem.at[1 - side], target("z", side))
+
+    def nc_copy(a, b):
+        return remote(NCS.at[a], NCR.at[1 - a, 1 - b],
+                      ncs_sem.at[a, b], ncr_sem.at[1 - a, 1 - b], corner(a, b))
+
+    def src_copy(side):
+        return remote(SRC.at[:, (CX - 1) * side], SXR.at[1 - side],
+                      ss_sem.at[side], sr_sem.at[1 - side], target("x", side))
+
+    def edge_copy(side):
+        return remote(EC, ECR.at[1 - side], es_sem.at[side], er_sem.at[1 - side], target("z", side))
+
+    def wall_x_copy(k, side):
+        return remote(WX.at[k], WXR.at[k, 1 - side],
+                      wxs_sem.at[k, side], wxr_sem.at[k, 1 - side], target("x", side))
+
+    def wall_z_copy(k, side):
+        return remote(WQ.at[k], WZR.at[k, 1 - side],
+                      wzs_sem.at[k, side], wzr_sem.at[k, 1 - side], target("z", side))
 
     def inv_copy(side):
         return pltpu.make_async_remote_copy(
@@ -82,6 +104,13 @@
             @pl.when(has[(axis, side)])
             def _():
                 act(side)
+
+    def corners(act):
+        for a in (0, 1):
+            for b in (0, 1):
+                @pl.when(has[("x", a)] & has[("z", b)])
+                def _():
+                    act(a, b)
 
     def exchange_start(phase):
         def send(i, carry):
@@ -121,32 +150,23 @@
         for m in range(8):
             ref[c, x, pl.ds(m, 8, stride=8), :] = rows[8 * m : 8 * m + 8]
 
-    def face_rows(low, high):
-        return jnp.where(half16, low, high)
-
-    def beside(low, high, before, after):
-        inner = pltpu.roll(jnp.where(half16, high, low), LANES // 2, 1)
-        zm = jnp.where(half16, pltpu.roll(before, LANES // 2, 1), inner)
-        zp = jnp.where(half16, inner, pltpu.roll(after, LANES // 2, 1))
-        return zm, zp
+    def face_rows(ref, c, low, high):
+        return jnp.where(half16, ref[c, pl.ds(0, CX), low, :], ref[c, pl.ds(0, CX), high, :])
+
+    def outer(before, after):
+        part = lax.broadcasted_iota(jnp.int32, before.shape, 1) < LANES // 2
+        return jnp.where(part, pltpu.roll(before, LANES // 2, 1), pltpu.roll(after, LANES // 2, 1))
 
     def z_first(row, tile):
-        return jnp.where(sub == 0, row, pltpu.roll(tile, 1, 0))
+        t = pltpu.roll(tile, 1, 0)
+        return jnp.where(sub == 0, jnp.where(half, row, pltpu.roll(t, LANES // 2, 1)), t)
 
     def z_last(row, tile):
-        return jnp.where(sub == 7, row, pltpu.roll(tile, 7, 0))
-
-    zero_plane = jnp.zeros((NY, LANES), F32)
-    for u in (UA, UB):
-        for c in range(3):
-            u[c, 0] = zero_plane
-            u[c, CX + 1] = zero_plane
-    NU[0, 0] = zero_plane
-    NU[0, CX + 1] = zero_plane
-    ZR[...] = jnp.zeros(ZR.shape, F32)
-    ZS[...] = jnp.zeros(ZS.shape, F32)
-    NZR[...] = jnp.zeros(NZR.shape, F32)
-    NZS[...] = jnp.zeros(NZS.shape, F32)
+        t = pltpu.roll(tile, 7, 0)
+        return jnp.where(sub == 7, jnp.where(half, pltpu.roll(t, LANES // 2, 1), row), t)
+
+    for ref in (XR, ZR, CR, NXR, NZR, NCR, SXR, ECR, WXR, WZR, CS, NCS):
+        ref[...] = jnp.zeros(ref.shape, F32)
     IR[...] = jnp.zeros(IR.shape, F32)
     IS[...] = jnp.zeros(IS.shape, F32)
     HR[...] = jnp.zeros(HR.shape, F32)
@@ -160,6 +180,7 @@
 
     lax.fori_loop(1, ndev, greet, 0)
     both("x", lambda side: pl.semaphore_signal(barrier, inc=1, device_id=target("x", side), device_id_type=MESH))
+    corners(lambda a, b: pl.semaphore_signal(barrier, inc=1, device_id=corner(a, b), device_id_type=MESH))
 
     def take(refs):
         def step(i, carry):
@@ -173,10 +194,18 @@
 
         lax.fori_loop(0, CX // 2, step, 0)
 
-    take([(nu_ref, 0, NU, 0, 1)] + [(vel_ref, c, UA, c, 1) for c in range(3)])
-    NZS[...] = face_rows(NU[0, pl.ds(1, CX), 0, :], NU[0, pl.ds(1, CX), NY - 1, :])
+    take([(nu_ref, 0, NU, 0, 0)] + [(vel_ref, c, UA, c, 0) for c in range(3)])
+
+    def send_corner(ref, rows):
+        ref[0, pl.ds(0, 1), :] = rows[0:1]
+        ref[1, pl.ds(0, 1), :] = rows[CX - 1 : CX]
+
+    NZS[...] = face_rows(NU, 0, 0, NY - 1)
+    send_corner(NCS, NZS[...])
     for c in range(3):
-        ZS[0, c] = face_rows(UA[c, pl.ds(1, CX), 0, :], UA[c, pl.ds(1, CX), NY - 1, :])
+        ZS[0, c, pl.ds(0, CX), :] = face_rows(UA, c, 0, NY - 1)
+        ZS[0, c, pl.ds(CX, CX), :] = face_rows(UA, c, 8, NY - 9)
+        send_corner(CS.at[0, c], ZS[0, c, pl.ds(0, CX), :])
     wet = nu_ref[0, :, 0, :]
     N2[...] = 2.0 * tall(jnp.concatenate([wet, wet, wet], axis=0)).T
     rows256 = lax.broadcasted_iota(jnp.int32, (8 * ndev, LANES), 0)
@@ -190,16 +219,21 @@
         IS[0, pl.ds(6 * a, 6), :] = inv_ref[a, :, 0, :]
         IS[1, pl.ds(6 * a, 6), :] = inv_ref[a, :, NB - 1, :]
 
-    others = (ndev - 1) + jnp.where(has[("x", 0)], 1, 0) + jnp.where(has[("x", 1)], 1, 0)
-    pl.semaphore_wait(barrier, others)
+    sides_x = jnp.where(has[("x", 0)], 1, 0) + jnp.where(has[("x", 1)], 1, 0)
+    sides_z = jnp.where(has[("z", 0)], 1, 0) + jnp.where(has[("z", 1)], 1, 0)
+    pl.semaphore_wait(barrier, (ndev - 1) + sides_x + sides_x * sides_z)
 
     both("x", lambda side: nu_copy(side).start())
     both("z", lambda side: nz_copy(side).start())
+    corners(lambda a, b: nc_copy(a, b).start())
     exchange_start(0)
     for c in range(3):
         both("x", lambda side: u_copy(0, c, side).start())
         both("z", lambda side: z_copy(0, c, side).start())
+        corners(lambda a, b: c_copy(0, c, a, b).start())
     both("z", lambda side: inv_copy(side).start())
+    take([(src_ref, c, SRC, c, 0) for c in range(3)])
+    both("x", lambda side: src_copy(side).start())
 
     SH[...] = jnp.zeros(SH.shape, F32)
     FORCE[...] = jnp.zeros(FORCE.shape, F32)
@@ -222,53 +256,118 @@
     def take_wall(k):
         exchange_wait(1 + k)
         wall = dot(ST[...], AR[1 + k].reshape(8 * ndev, LANES))
+        WQ[k] = wall[:ROWS]
+        both("z", lambda side: wall_z_copy(k, side).start())
         WT[...] = wall.T
-        tiles = [
-            jnp.where(
+        for j in range(8):
+            WX[k, pl.ds(8 * j, 8), :] = jnp.where(
                 half,
                 WT[pl.ds(j, 8, stride=8), :],
                 pltpu.roll(WT[pl.ds(NY + j, 8, stride=8), :], LANES // 2, 1))
-            for j in range(8)
-        ]
-        for q in range(ROWS):
-            c, x = q // CX, q % CX
-            for j in range(8):
-                rows = pl.ds(8 * j, 8)
-                wall = pltpu.roll(tiles[j], LANES - q, 1) if q else tiles[j]
-                RW[c, x, rows, :] = RHS[c, x, rows, :] + CW[x, rows, :] * wall
+        both("x", lambda side: wall_x_copy(k, side).start())
+        tiles = [WX[k, pl.ds(8 * j, 8), :] for j in range(8)]
+        for c in range(3):
+            for x in range(CX):
+                add_wall(c, x, c * CX + x, tiles)
+
+    def add_wall(c, x, q, tiles):
+        for j in range(8):
+            rows = pl.ds(8 * j, 8)
+            wall = pltpu.roll(tiles[j], LANES - q, 1) if q else tiles[j]
+            RW[c, x + 1, rows, :] = RHS[c, x + 1, rows, :] + CW[x + 1, rows, :] * wall
+
+    def take_wall_halo(k):
+        both("z", lambda side: wall_z_copy(k, side).wait_send())
+        both("z", lambda side: wall_z_copy(k, 1 - side).wait_recv())
+        both("x", lambda side: wall_x_copy(k, side).wait_send())
+        both("x", lambda side: wall_x_copy(k, 1 - side).wait_recv())
+        for c in range(3):
+            rows = pl.ds(CX * c, CX)
+            wall = jnp.where(half16, pltpu.roll(WZR[k, 0, rows, :], 1, 1), pltpu.roll(WZR[k, 1, rows, :], LANES // 2, 1))
+            RH[c] = HC[7 + c] + HC[6] * wall
+        for side, x, own in ((0, -1, CX - 1), (1, CX, 0)):
+            tiles = [WXR[k, side, pl.ds(8 * j, 8), :] for j in range(8)]
+            for c in range(3):
+                add_wall(c, x, c * CX + own, tiles)
 
     send_wall(0)
-    take([(src_ref, c, RHS, c, 0) for c in range(3)])
 
     both("x", lambda side: nu_copy(side).wait_send())
     both("x", lambda side: nu_copy(1 - side).wait_recv())
     both("z", lambda side: nz_copy(side).wait_send())
     both("z", lambda side: nz_copy(1 - side).wait_recv())
-    nzm, nzp = beside(NU[0, pl.ds(1, CX), 0, :], NU[0, pl.ds(1, CX), NY - 1, :], NZR[0], NZR[1])
+    corners(lambda a, b: nc_copy(a, b).wait_send())
+    corners(lambda a, b: nc_copy(1 - a, 1 - b).wait_recv())
+    both("x", lambda side: src_copy(side).wait_send())
+    both("x", lambda side: src_copy(1 - side).wait_recv())
     y_first = lane % NY == 0
     y_last = lane % NY == NY - 1
-    for x in range(CX):
-        tiles = [NU[0, x + 1, pl.ds(8 * j, 8), :] for j in range(8)]
+    nu_rows = outer(NZR[0], NZR[1])
+
+    def halo_planes(ref, c, near):
+        def get(x, j):
+            rows = pl.ds(8 * j, 8)
+            if x < 0:
+                return near(0, x + 2, rows)
+            if x >= CX:
+                return near(1, x - CX, rows)
+            return ref[c, x, rows, :]
+        return get
+
+    get_nu = halo_planes(NU, 0, lambda side, n, rows: NXR[side, n, rows, :])
+
+    def coefficients(x, row, valid):
+        tiles = [get_nu(x, j) for j in range(8)]
         for j in range(8):
             rows = pl.ds(8 * j, 8)
             t = tiles[j]
-            zm = tiles[j - 1] if j else z_first(nzm[x : x + 1], tiles[7])
-            zp = tiles[j + 1] if j < 7 else z_last(nzp[x : x + 1], tiles[0])
+            zm = tiles[j - 1] if j else z_first(row, tiles[7])
+            zp = tiles[j + 1] if j < 7 else z_last(row, tiles[0])
             ym = jnp.where(y_first, t, pltpu.roll(t, 1, 1))
             yp = jnp.where(y_last, t, pltpu.roll(t, LANES - 1, 1))
-            faces = [0.5 * (t + o) for o in (NU[0, x, rows, :], NU[0, x + 2, rows, :], zm, zp, ym, yp)]
+            faces = [0.5 * (t + o) for o in (get_nu(x - 1, j), get_nu(x + 1, j), zm, zp, ym, yp)]
             total = 1.0 + faces[0]
             for f in faces[1:]:
                 total = total + f
-            inverse = 1.0 / total
+            inverse = valid / total
             for n in range(4):
-                CF[n, x, rows, :] = faces[n] * inverse
+                CF[n, x + 1, rows, :] = faces[n] * inverse
             below = faces[4] * inverse
-            CW[x, rows, :] = jnp.where(y_first, below, 0.0)
-            CF[4, x, rows, :] = jnp.where(y_first, 0.0, below)
-            CF[5, x, rows, :] = jnp.where(y_last, 0.0, faces[5] * inverse)
+            CW[x + 1, rows, :] = jnp.where(y_first, below, 0.0)
+            CF[4, x + 1, rows, :] = jnp.where(y_first, 0.0, below)
+            CF[5, x + 1, rows, :] = jnp.where(y_last, 0.0, faces[5] * inverse)
             for c in range(3):
-                RHS[c, x, rows, :] = RHS[c, x, rows, :] * inverse
+                if x < 0:
+                    base = SXR[0, c, rows, :]
+                elif x >= CX:
+                    base = SXR[1, c, rows, :]
+                else:
+                    base = SRC[c, x, rows, :]
+                RHS[c, x + 1, rows, :] = base * inverse
+
+    for x in range(CX):
+        coefficients(x, nu_rows[x : x + 1], 1.0)
+
+    def edge_rows(ref, n, m):
+        return jnp.where(half16, ref[n, pl.ds(1, CX), 0, :], ref[m, pl.ds(1, CX), NY - 1, :])
+
+    for i, (n, m) in enumerate(((0, 0), (1, 1), (3, 2), (2, 3), (4, 4), (5, 5))):
+        EC[i] = edge_rows(CF, n, m)
+    EC[6] = jnp.where(half16, CW[pl.ds(1, CX), 0, :], CW[pl.ds(1, CX), NY - 1, :])
+    for c in range(3):
+        EC[7 + c] = edge_rows(RHS, c, c)
+    both("z", lambda side: edge_copy(side).start())
+
+    one_row = lax.broadcasted_iota(jnp.int32, (1, LANES), 1) < LANES // 2
+    for side, x in ((0, -1), (1, CX)):
+        row = outer(NCR[side, 0, pl.ds(0, 8), :], NCR[side, 1, pl.ds(0, 8), :])[0:1]
+        coefficients(x, row, jnp.where(has[("x", side)], 1.0, 0.0))
+
+    def take_edges():
+        both("z", lambda side: edge_copy(side).wait_send())
+        both("z", lambda side: edge_copy(1 - side).wait_recv())
+        for i in range(10):
+            HC[i] = outer(ECR[0, i], ECR[1, i])
 
     both("z", lambda side: inv_copy(side).wait_send())
     both("z", lambda side: inv_copy(1 - side).wait_recv())
@@ -278,57 +377,126 @@
             INV[n, pl.ds(0, NB), :] = inv_ref[a, b]
             INV[n, pl.ds(NB, 8), :] = ends(IR[1, pl.ds(n, 1), :], IR[0, pl.ds(n, 1), :])
 
-    def plane(c, x, old, new, zms, zps):
-        tiles = [old[c, x + 1, pl.ds(8 * j, 8), :] for j in range(8)]
+    def plane(c, x, get, put, row):
+        tiles = [get(x, j) for j in range(8)]
         for j in range(8):
             rows = pl.ds(8 * j, 8)
             t = tiles[j]
-            zm = tiles[j - 1] if j else z_first(zms[x : x + 1], tiles[7])
-            zp = tiles[j + 1] if j < 7 else z_last(zps[x : x + 1], tiles[0])
-            num = RW[c, x, rows, :] + CF[0, x, rows, :] * old[c, x, rows, :]
-            num = num + CF[1, x, rows, :] * old[c, x + 2, rows, :]
-            num = num + CF[2, x, rows, :] * zm + CF[3, x, rows, :] * zp
-            ys = CF[4, x, rows, :] * pltpu.roll(t, 1, 1) + CF[5, x, rows, :] * pltpu.roll(t, LANES - 1, 1)
-            new[c, x + 1, rows, :] = num + ys
-
-    last = SUBITERS * SWEEPS
-
-    def level(k, slot):
-        old, new = ((UB, UA), (UA, UB))[slot]
+            zm = tiles[j - 1] if j else z_first(row, tiles[7])
+            zp = tiles[j + 1] if j < 7 else z_last(row, tiles[0])
+            num = RW[c, x + 1, rows, :] + CF[0, x + 1, rows, :] * get(x - 1, j)
+            num = num + CF[1, x + 1, rows, :] * get(x + 1, j)
+            num = num + CF[2, x + 1, rows, :] * zm + CF[3, x + 1, rows, :] * zp
+            ys = CF[4, x + 1, rows, :] * pltpu.roll(t, 1, 1)
+            ys = ys + CF[5, x + 1, rows, :] * pltpu.roll(t, LANES - 1, 1)
+            put(x, rows, num + ys)
+
+    sub16 = lax.broadcasted_iota(jnp.int32, (CX, LANES), 0)
+    last = SUBITERS * SWEEPS // 2
+
+    def arrive(p, c):
+        both("z", lambda side: z_copy(p, c, 1 - side).wait_recv())
+        both("x", lambda side: u_copy(p, c, 1 - side).wait_recv())
+        corners(lambda a, b: c_copy(p, c, 1 - a, 1 - b).wait_recv())
+
+    def beside(p, c):
+        near = outer(ZR[p, c, 0, pl.ds(0, CX), :], ZR[p, c, 1, pl.ds(0, CX), :])
+        far = outer(ZR[p, c, 0, pl.ds(CX, CX), :], ZR[p, c, 1, pl.ds(CX, CX), :])
+        low = outer(CR[p, c, 0, 0], CR[p, c, 0, 1])[0:1]
+        high = outer(CR[p, c, 1, 0], CR[p, c, 1, 1])[0:1]
+        return near, far, low, high
+
+    def even(p, c):
+        return halo_planes(UA, c, lambda side, n, rows: XR[p, c, side, n, rows, :])
+
+    def odd(c):
+        return lambda x, j: UB[c, x + 1, pl.ds(8 * j, 8), :]
+
+    def put_odd(c):
+        def put(x, rows, value):
+            UB[c, x + 1, rows, :] = value
+        return put
+
+    def put_even(c):
+        def put(x, rows, value):
+            UA[c, x, rows, :] = value
+        return put
+
+    def middle(p, c, xs, rows):
+        near, far, low, high = rows
+        for x in xs:
+            row = low if x < 0 else high if x >= CX else near[x : x + 1]
+            plane(c, x, even(p, c), put_odd(c), row)
+
+    def middle_rows(p, c, rows):
+        near, far, low, high = rows
+        before = jnp.where(sub16 == 0, low, pltpu.roll(near, 1, 0))
+        after = jnp.where(sub16 == CX - 1, high, pltpu.roll(near, CX - 1, 0))
+        total = RH[c] + HC[0] * before + HC[1] * after + HC[2] * far
+        total = total + HC[3] * ZS[p, c, pl.ds(0, CX), :]
+        return total + HC[4] * pltpu.roll(near, 1, 1) + HC[5] * pltpu.roll(near, LANES - 1, 1)
+
+    def finish(n, p, c, rows, xs):
+        near = middle_rows(p, c, rows)
+
+        def final(group):
+            for x in group:
+                plane(c, x, odd(c), put_even(c), near[x : x + 1])
+
+        both("x", lambda side: u_copy(p, c, side).wait_send())
+        corners(lambda a, b: c_copy(p, c, a, b).wait_send())
+        both("z", lambda side: z_copy(p, c, side).wait_send())
+        final((0, 1, CX - 1, CX - 2))
+        edge = [
+            jnp.where(one_row, UA[c, x, pl.ds(0, 1), :], UA[c, x, pl.ds(NY - 1, 1), :]) for x in (0, CX - 1)]
+        CS[1 - p, c, 0, pl.ds(0, 1), :] = edge[0]
+        CS[1 - p, c, 1, pl.ds(0, 1), :] = edge[1]
+
+        @pl.when(n + 1 < last)
+        def _():
+            both("x", lambda side: u_copy(1 - p, c, side).start())
+            corners(lambda a, b: c_copy(1 - p, c, a, b).start())
+
+        middle(p, c, xs, rows)
+        final(range(2, CX - 2))
+        ZS[1 - p, c, pl.ds(0, CX), :] = face_rows(UA, c, 0, NY - 1)
+        ZS[1 - p, c, pl.ds(CX, CX), :] = face_rows(UA, c, 8, NY - 9)
+
+        @pl.when(n + 1 < last)
+        def _():
+            both("z", lambda side: z_copy(1 - p, c, side).start())
+
+    def first_pair(k):
+        n = k * (SWEEPS // 2)
+        p = lax.rem(n, 2)
+
+        def start(c, carry):
+            arrive(p, c)
+            middle(p, c, range(CX), beside(p, c))
+            return carry
+
+        lax.fori_loop(0, 3, start, 0)
+        take_wall_halo(k)
+
+        def rest(c, carry):
+            rows = beside(p, c)
+            middle(p, c, (-1, CX), rows)
+            finish(n, p, c, rows, ())
+            return carry
+
+        lax.fori_loop(0, 3, rest, 0)
+
+    def pair(n, carry):
+        p = lax.rem(n, 2)
 
         def component(c, carry):
-            both("z", lambda side: z_copy(1 - slot, c, 1 - side).wait_recv())
-            zms, zps = beside(
-                old[c, pl.ds(1, CX), 0, :], old[c, pl.ds(1, CX), NY - 1, :],
-                ZR[1 - slot, c, 0], ZR[1 - slot, c, 1])
-            both("x", lambda side: u_copy(1 - slot, c, 1 - side).wait_recv())
-
-            @pl.when(k >= 2)
-            def _():
-                both("x", lambda side: u_copy(slot, c, side).wait_send())
-                both("z", lambda side: z_copy(slot, c, side).wait_send())
-
-            plane(c, 0, old, new, zms, zps)
-            plane(c, CX - 1, old, new, zms, zps)
-
-            @pl.when(k < last)
-            def _():
-                both("x", lambda side: u_copy(slot, c, side).start())
-
-            for x in range(1, CX - 1):
-                plane(c, x, old, new, zms, zps)
-            ZS[slot, c] = face_rows(new[c, pl.ds(1, CX), 0, :], new[c, pl.ds(1, CX), NY - 1, :])
-
-            @pl.when(k < last)
-            def _():
-                both("z", lambda side: z_copy(slot, c, side).start())
+            arrive(p, c)
+            rows = beside(p, c)
+            middle(p, c, (-1, 0, 1, 2, CX, CX - 1, CX - 2, CX - 3), rows)
+            finish(n, p, c, rows, range(3, CX - 3))
             return carry
 
         lax.fori_loop(0, 3, component, 0)
-
-    def levels(n, carry):
-        level(2 * n + 1, 1)
-        level(2 * n + 2, 0)
         return carry
 
     def shell_sweep(step, carry):
@@ -350,12 +518,13 @@
 
     def subiteration(k, carry):
         take_wall(k)
-        lax.fori_loop(k * (SWEEPS // 2), (k + 1) * (SWEEPS // 2), levels, 0)
+        first_pair(k)
+        lax.fori_loop(k * (SWEEPS // 2) + 1, (k + 1) * (SWEEPS // 2), pair, 0)
         tiles = [jnp.zeros((8, LANES), F32) for j in range(8)]
         for q in range(ROWS):
             here = (lane == q) | (lane == q + NY)
             for j in range(8):
-                tile = UA[q // CX, q % CX + 1, pl.ds(8 * j, 8), :]
+                tile = UA[q // CX, q % CX, pl.ds(8 * j, 8), :]
                 tiles[j] = jnp.where(here, pltpu.roll(tile, q, 1) if q else tile, tiles[j])
         for j in range(8):
             PULL[pl.ds(j, 8, stride=8), :] = jnp.where(half, tiles[j], 0.0)
@@ -387,6 +556,7 @@
             send_wall(k + 1)
         return carry
 
+    take_edges()
     lax.fori_loop(0, SUBITERS, subiteration, 0)
 
     for f in range(6):
@@ -395,7 +565,7 @@
     def give(i, carry):
         for c in range(3):
             rows = jnp.concatenate(
-                [UA[c, 2 * i + 1 + p, pl.ds(m, 8, stride=8), :] for p in range(2) for m in range(8)], axis=0).T
+                [UA[c, 2 * i + p, pl.ds(m, 8, stride=8), :] for p in range(2) for m in range(8)], axis=0).T
             for n in range(8):
                 top, low = rows[8 * n : 8 * n + 8], rows[NY + 8 * n : NY + 8 * n + 8]
                 uout_ref[c, 2 * i, pl.ds(8 * n, 8), :] = jnp.where(half, top, pltpu.roll(low, LANES // 2, 1))
@@ -403,10 +573,6 @@
         return carry
 
     lax.fori_loop(0, CX // 2, give, 0)
-    for c in range(3):
-        both("x", lambda side: u_copy(1, c, side).wait_send())
-        both("z", lambda side: z_copy(1, c, side).wait_send())
-
 
 def body(velocity, source, viscosity, owners, targets, shell_load, shell_state, shell_inverse):
     nsec = lax.axis_size("sec")
@@ -431,17 +597,29 @@
         in_specs=[vmem] * 8,
         out_specs=(vmem, vmem),
         scratch_shapes=[
+            pltpu.VMEM((3, CX, NY, LANES), F32),
+            pltpu.VMEM((3, CX + 2, NY, LANES), F32),
+            pltpu.VMEM((1, CX, NY, LANES), F32),
+            pltpu.VMEM((6, CX + 2, NY, LANES), F32),
+            pltpu.VMEM((CX + 2, NY, LANES), F32),
+            pltpu.VMEM((3, CX, NY, LANES), F32),
             pltpu.VMEM((3, CX + 2, NY, LANES), F32),
             pltpu.VMEM((3, CX + 2, NY, LANES), F32),
-            pltpu.VMEM((1, CX + 2, NY, LANES), F32),
-            pltpu.VMEM((6, CX, NY, LANES), F32),
-            pltpu.VMEM((CX, NY, LANES), F32),
-            pltpu.VMEM((3, CX, NY, LANES), F32),
-            pltpu.VMEM((3, CX, NY, LANES), F32),
-            pltpu.VMEM((2, 3, CX, LANES), F32),
-            pltpu.VMEM((2, 3, 2, CX, LANES), F32),
+            pltpu.VMEM((2, 3, 2, 2, NY, LANES), F32),
+            pltpu.VMEM((2, 3, 2 * CX, LANES), F32),
+            pltpu.VMEM((2, 3, 2, 2 * CX, LANES), F32),
+            pltpu.VMEM((2, 3, 2, 8, LANES), F32),
+            pltpu.VMEM((2, 3, 2, 2, 8, LANES), F32),
+            pltpu.VMEM((2, 2, NY, LANES), F32),
             pltpu.VMEM((CX, LANES), F32),
             pltpu.VMEM((2, CX, LANES), F32),
+            pltpu.VMEM((2, 8, LANES), F32),
+            pltpu.VMEM((2, 2, 8, LANES), F32),
+            pltpu.VMEM((2, 3, NY, LANES), F32),
+            pltpu.VMEM((10, CX, LANES), F32),
+            pltpu.VMEM((2, 10, CX, LANES), F32),
+            pltpu.VMEM((10, CX, LANES), F32),
+            pltpu.VMEM((3, CX, LANES), F32),
             pltpu.VMEM((8 * ndev, LANES), F32),
             pltpu.VMEM((LANES, 8 * ndev), F32),
             pltpu.VMEM((8 * ndev, LANES), F32),
@@ -449,6 +627,10 @@
             pltpu.VMEM((5, ndev, 8, LANES), F32),
             pltpu.VMEM((5, ndev, 8, LANES), F32),
             pltpu.VMEM((LANES, LANES), F32),
+            pltpu.VMEM((2, ROWS, LANES), F32),
+            pltpu.VMEM((2, NY, LANES), F32),
+            pltpu.VMEM((2, 2, NY, LANES), F32),
+            pltpu.VMEM((2, 2, ROWS, LANES), F32),
             pltpu.VMEM((LANES, LANES), F32),
             pltpu.VMEM((LANES, LANES), F32),
             pltpu.VMEM((6, 24, LANES), F32),
@@ -459,7 +641,10 @@
             pltpu.VMEM((2, 2, 16, LANES), F32),
             pltpu.VMEM((2, 2, 16, LANES), F32),
             dma((2, 3, 2)), dma((2, 3, 2)), dma((2, 3, 2)), dma((2, 3, 2)),
+            dma((2, 3, 2, 2)), dma((2, 3, 2, 2)),
+            dma((2,)), dma((2,)), dma((2,)), dma((2,)), dma((2, 2)), dma((2, 2)),
             dma((2,)), dma((2,)), dma((2,)), dma((2,)),
+            dma((2, 2)), dma((2, 2)), dma((2, 2)), dma((2, 2)),
             dma((5,)), dma((5,)),
             dma((2,)), dma((2,)), dma((2, 2)), dma((2, 2)),
         ],

time: 114 us -> 109 us (0.956)
  Pallas kernels: 103 us -> 97.8 us
    pallas_call x1, Pallas kernels: 103 us -> 97.8 us  [body(): pl.pallas_call(lambda *refs: kernel(nsec, ndev, *refs), out_shape=(jax.Sh...]
where the time goes in v4:
time: 109 us
  Pallas kernels  97.8 us (90%)
  local copies, waits for them, and re-layouts  7.63 us (7%)
  other arithmetic  2.87 us (3%)
    pallas_call x1, Pallas kernels, body(): pl.pallas_call(lambda *refs: kernel(nsec, ndev, *refs), out_shape=(jax.Sh...  97.8 us
    unnamed x8, local copies, waits for them, and re-layouts  5.64 us

profile of v4, /device:TPU:8, one launch (start us, length us, event | category | flops | bytes accessed | tf_op | source)
XLA Modules:
  0.0 108.9 jit_solution(35314879919822483)
XLA Ops:
  0.6 0.8 select_reduce_fusion
  1.4 0.7 broadcast_add_fusion.3
  2.1 0.7 broadcast_add_fusion.1
  2.8 0.7 fusion.2
  3.5 0.9 copy_bitcast_fusion.1
  4.4 1.1 %reshape.28.refs_7_ = f32[6,6,16,128]{3,2,1,0:T(8,128)S(1)} reshape(f32[6,6,2048]{2,1,0:T(8,128)} %param.15) | data formatting | bytes 589824 | tf_op jit(solution)/shard_map/reshape | solution.py:656
  5.5 0.0 copy-start
  5.5 1.4 %copy-done = f32[3,16,64,128]{3,2,1,0:T(8,128)S(1)} copy-done((f32[3,16,64,128]{3,2,1,0:T(8,128)S(1)}, f32[3,16,64,128]{3,2,1,0:T(8,128)}, u32[]{:S(2)}) %copy-start) | copy-done | bytes 1572888
  6.9 0.0 copy-start.1
  6.9 1.4 %copy-done.1 = f32[3,16,64,128]{3,2,1,0:T(8,128)S(1)} copy-done((f32[3,16,64,128]{3,2,1,0:T(8,128)S(1)}, f32[3,16,64,128]{3,2,1,0:T(8,128)}, u32[]{:S(2)}) %copy-start.1) | copy-done | bytes 1572888
  8.3 0.0 copy-start.2
  8.3 1.0 copy-done.2
  9.4 97.8 %shard_map.95 = (f32[3,16,64,128]{3,2,1,0:T(8,128)S(1)}, f32[6,16,128]{2,1,0:T(8,128)S(1)}) custom-call(f32[3,16,64,128]{3,2,1,0:T(8,128)S(1)} %copy-done, f32[3,16,64,128]{3,2,1,0:T(8,128)S(1)} %copy-done.1, f32[1,16,64,128]{3,2,1,0:T(8,128)S(1)} %bitcast.21, s32[1,128]{1,0:T(1,128)S(1)} %get-tuple-element.9.refs_3_, ...), custom_call_target="tpu_custom_call" | custom-call | tf_op jit(solution)/shard_map/pallas_call | solution.py:591
  107.1 0.6 copy.16
  107.8 1.1 %copy.18 = f32[3,16,64,128]{3,2,1,0:T(8,128)} copy(f32[3,16,64,128]{3,2,1,0:T(8,128)S(1)} %get-tuple-element.17) | data formatting | bytes 3145728
  (1 shorter events, 0.0 us)
Async XLA Ops:
  5.5 1.4 %copy-start = (f32[3,16,64,128]{3,2,1,0:T(8,128)S(1)}, f32[3,16,64,128]{3,2,1,0:T(8,128)}, u32[]{:S(2)}) copy-start(f32[3,16,64,128]{3,2,1,0:T(8,128)} %refs_0_.1) | copy-start | bytes 4718596
  6.9 1.4 %copy-start.1 = (f32[3,16,64,128]{3,2,1,0:T(8,128)S(1)}, f32[3,16,64,128]{3,2,1,0:T(8,128)}, u32[]{:S(2)}) copy-start(f32[3,16,64,128]{3,2,1,0:T(8,128)} %refs_1_.1) | copy-start | bytes 4718596
  8.3 1.0 copy-start.2

commit v5 on v4

--- a/solution.py
+++ b/solution.py
@@ -15,21 +15,21 @@
 ROWS = 3 * CX
 MESH = pl.DeviceIdType.MESH
 F32 = jnp.float32
-HIGHEST = lax.Precision.HIGHEST
 
 
 def kernel(
     nsec, ndev,
-    vel_ref, src_ref, nu_ref, key_ref, tgt_ref, load_ref, state_ref, inv_ref,
+    vel_hbm, src_hbm, nu_hbm, owner_ref, name_ref, load_hbm, state_hbm, inv_hbm,
     uout_ref, sout_ref,
+    vel_ref, src_ref, nu_ref, load_ref, state_ref, inv_ref,
     UA, UB, NU, CF, CW, SRC, RHS, RW, XR, ZS, ZR, CS, CR,
     NXR, NZS, NZR, NCS, NCR, SXR, EC, ECR, HC, RH,
     S, ST, G, GT, AS, AR, WT, WQ, WX, WXR, WZR, PULL, N2,
-    SH, FORCE, INV, IS, IR, HS, HR,
+    SH, LOAD, FORCE, INV, IS, IR, HS, HR,
     xs_sem, xr_sem, zs_sem, zr_sem, cs_sem, cr_sem,
     nxs_sem, nxr_sem, nzs_sem, nzr_sem, ncs_sem, ncr_sem, ss_sem, sr_sem, es_sem, er_sem,
     wxs_sem, wxr_sem, wzs_sem, wzr_sem,
-    as_sem, ar_sem, is_sem, ir_sem, hs_sem, hr_sem,
+    as_sem, ar_sem, is_sem, ir_sem, hs_sem, hr_sem, in_sem,
 ):
     sec = lax.axis_index("sec")
     dev = lax.axis_index("dev")
@@ -132,8 +132,14 @@
         copy.wait_send()
         copy.wait_recv()
 
-    def dot(a, b):
-        return lax.dot_general(a, b, (((1,), (0,)), ((), ())), precision=HIGHEST, preferred_element_type=F32)
+    def pick(one_hot, b):
+        high = b.astype(jnp.bfloat16)
+        rest = b - high.astype(F32)
+        middle = rest.astype(jnp.bfloat16)
+        low = (rest - middle.astype(F32)).astype(jnp.bfloat16)
+        parts = jnp.concatenate([high, middle, low], axis=1)
+        out = lax.dot_general(one_hot, parts, (((1,), (0,)), ((), ())), preferred_element_type=F32)
+        return (out[:, :LANES] + out[:, LANES : 2 * LANES]) + out[:, 2 * LANES :]
 
     def tall(rows):
         return jnp.concatenate([rows, jnp.zeros((LANES - ROWS, LANES), F32)], axis=0)
@@ -164,6 +170,14 @@
     def z_last(row, tile):
         t = pltpu.roll(tile, 7, 0)
         return jnp.where(sub == 7, jnp.where(half, pltpu.roll(t, LANES // 2, 1), row), t)
+
+    loads = [
+        pltpu.make_async_copy(src, dst, in_sem.at[n])
+        for n, (src, dst) in enumerate((
+            (state_hbm, state_ref), (nu_hbm, nu_ref), (vel_hbm, vel_ref),
+            (src_hbm, src_ref), (inv_hbm, inv_ref), (load_hbm, load_ref)))]
+    for copy in loads:
+        copy.start()
 
     for ref in (XR, ZR, CR, NXR, NZR, NCR, SXR, ECR, WXR, WZR, CS, NCS):
         ref[...] = jnp.zeros(ref.shape, F32)
@@ -182,80 +196,94 @@
     both("x", lambda side: pl.semaphore_signal(barrier, inc=1, device_id=target("x", side), device_id_type=MESH))
     corners(lambda a, b: pl.semaphore_signal(barrier, inc=1, device_id=corner(a, b), device_id_type=MESH))
 
+    place16 = lax.broadcasted_iota(jnp.int32, (CX, CX), 0)
+    other16 = lax.broadcasted_iota(jnp.int32, (CX, CX), 1)
+
+    def column(row):
+        return jnp.sum(jnp.where(place16 == other16, jnp.broadcast_to(row, (CX, CX)), 0.0), axis=1, keepdims=True)
+
+    owner_row = owner_ref[...].astype(F32)
+    owner = column(owner_row)
+    name = column(name_ref[...].astype(F32))
+    same = (owner == owner_row) & (other16 < place16)
+    rank = jnp.sum(jnp.where(same, 1.0, 0.0), axis=1, keepdims=True)
+    slots = lax.broadcasted_iota(jnp.int32, (CX, 8 * ndev), 1).astype(F32)
+    blocks = lax.broadcasted_iota(jnp.int32, (CX, LANES), 1).astype(F32)
+    key = 8.0 * owner + rank
+    one_hot = jnp.concatenate(
+        [jnp.where(slots == key + 2.0 * c, 1.0, 0.0) for c in range(3)]
+        + [jnp.zeros((LANES - ROWS, 8 * ndev), F32)], axis=0)
+    names = tall(jnp.concatenate(
+        [jnp.where(blocks == name + float(NB * c), 1.0, 0.0) for c in range(3)], axis=0))
+    ST[...] = one_hot.astype(jnp.bfloat16)
+    S[...] = one_hot.T.astype(jnp.bfloat16)
+    AS[0] = lax.dot_general(
+        S[...], names.astype(jnp.bfloat16), (((1,), (0,)), ((), ())), preferred_element_type=F32
+    ).reshape(ndev, 8, LANES)
+
+    sides_x = jnp.where(has[("x", 0)], 1, 0) + jnp.where(has[("x", 1)], 1, 0)
+    sides_z = jnp.where(has[("z", 0)], 1, 0) + jnp.where(has[("z", 1)], 1, 0)
+    pl.semaphore_wait(barrier, (ndev - 1) + sides_x + sides_x * sides_z)
+    exchange_start(0)
+
     def take(refs):
         def step(i, carry):
-            for ref, c, out, d, shift in refs:
+            for ref, c, out, d in refs:
                 first = [ref[c, 2 * i, pl.ds(8 * n, 8), :] for n in range(8)]
                 second = [ref[c, 2 * i + 1, pl.ds(8 * n, 8), :] for n in range(8)]
                 rows = turn(first, second)
-                spread(out, d, 2 * i + shift, rows[:NY])
-                spread(out, d, 2 * i + 1 + shift, rows[NY:])
+                spread(out, d, 2 * i, rows[:NY])
+                spread(out, d, 2 * i + 1, rows[NY:])
             return carry
 
         lax.fori_loop(0, CX // 2, step, 0)
-
-    take([(nu_ref, 0, NU, 0, 0)] + [(vel_ref, c, UA, c, 0) for c in range(3)])
 
     def send_corner(ref, rows):
         ref[0, pl.ds(0, 1), :] = rows[0:1]
         ref[1, pl.ds(0, 1), :] = rows[CX - 1 : CX]
 
+    loads[1].wait()
+    take([(nu_ref, 0, NU, 0)])
     NZS[...] = face_rows(NU, 0, 0, NY - 1)
     send_corner(NCS, NZS[...])
+    corners(lambda a, b: nc_copy(a, b).start())
+    both("z", lambda side: nz_copy(side).start())
+    both("x", lambda side: nu_copy(side).start())
+    wet = nu_ref[0, :, 0, :]
+    N2[...] = 2.0 * tall(jnp.concatenate([wet, wet, wet], axis=0)).T
+
+    loads[2].wait()
+    take([(vel_ref, c, UA, c) for c in range(3)])
     for c in range(3):
         ZS[0, c, pl.ds(0, CX), :] = face_rows(UA, c, 0, NY - 1)
         ZS[0, c, pl.ds(CX, CX), :] = face_rows(UA, c, 8, NY - 9)
         send_corner(CS.at[0, c], ZS[0, c, pl.ds(0, CX), :])
-    wet = nu_ref[0, :, 0, :]
-    N2[...] = 2.0 * tall(jnp.concatenate([wet, wet, wet], axis=0)).T
-    rows256 = lax.broadcasted_iota(jnp.int32, (8 * ndev, LANES), 0)
-    one_hot = jnp.where(rows256 == key_ref[...], 1.0, 0.0).astype(F32)
-    S[...] = one_hot
-    ST[...] = one_hot.T
-    rows128 = lax.broadcasted_iota(jnp.int32, (LANES, LANES), 0)
-    names = jnp.where(rows128 == tgt_ref[...], 1.0, 0.0).astype(F32)
-    AS[0] = dot(one_hot, names.T).reshape(ndev, 8, LANES)
-    for a in range(6):
-        IS[0, pl.ds(6 * a, 6), :] = inv_ref[a, :, 0, :]
-        IS[1, pl.ds(6 * a, 6), :] = inv_ref[a, :, NB - 1, :]
-
-    sides_x = jnp.where(has[("x", 0)], 1, 0) + jnp.where(has[("x", 1)], 1, 0)
-    sides_z = jnp.where(has[("z", 0)], 1, 0) + jnp.where(has[("z", 1)], 1, 0)
-    pl.semaphore_wait(barrier, (ndev - 1) + sides_x + sides_x * sides_z)
-
-    both("x", lambda side: nu_copy(side).start())
-    both("z", lambda side: nz_copy(side).start())
-    corners(lambda a, b: nc_copy(a, b).start())
-    exchange_start(0)
-    for c in range(3):
+        corners(lambda a, b: c_copy(0, c, a, b).start())
+        both("z", lambda side: z_copy(0, c, side).start())
         both("x", lambda side: u_copy(0, c, side).start())
-        both("z", lambda side: z_copy(0, c, side).start())
-        corners(lambda a, b: c_copy(0, c, a, b).start())
-    both("z", lambda side: inv_copy(side).start())
-    take([(src_ref, c, SRC, c, 0) for c in range(3)])
-    both("x", lambda side: src_copy(side).start())
-
+
+    loads[0].wait()
     SH[...] = jnp.zeros(SH.shape, F32)
     FORCE[...] = jnp.zeros(FORCE.shape, F32)
-    for f in range(6):
-        SH[f, pl.ds(0, NB), :] = state_ref[f]
+    for n in range(NB):
+        SH[:, n, :] = state_ref[:, pl.ds(LANES * n, LANES)]
 
     def ends(right, left):
         return jnp.where(sub == 0, right, jnp.where(sub == 7, left, 0.0))
 
     exchange_wait(0)
     got = AR[0].reshape(8 * ndev, LANES)
-    G[...] = got
-    GT[...] = got.T
+    G[...] = got.astype(jnp.bfloat16)
+    GT[...] = got.T.astype(jnp.bfloat16)
 
     def send_wall(k):
         rows = jnp.concatenate([SH[f, pl.ds(0, NB), :] for f in range(3)], axis=0)
-        AS[1 + k] = dot(G[...], tall(rows)).reshape(ndev, 8, LANES)
+        AS[1 + k] = pick(G[...], tall(rows)).reshape(ndev, 8, LANES)
         exchange_start(1 + k)
 
     def take_wall(k):
         exchange_wait(1 + k)
-        wall = dot(ST[...], AR[1 + k].reshape(8 * ndev, LANES))
+        wall = pick(ST[...], AR[1 + k].reshape(8 * ndev, LANES))
         WQ[k] = wall[:ROWS]
         both("z", lambda side: wall_z_copy(k, side).start())
         WT[...] = wall.T
@@ -268,13 +296,18 @@
         tiles = [WX[k, pl.ds(8 * j, 8), :] for j in range(8)]
         for c in range(3):
             for x in range(CX):
-                add_wall(c, x, c * CX + x, tiles)
+                for j, value in enumerate(add_wall(c, x, c * CX + x, tiles)):
+                    rows = pl.ds(8 * j, 8)
+                    UB[c, x + 1, rows, :] = UB[c, x + 1, rows, :] + value
 
     def add_wall(c, x, q, tiles):
+        values = []
         for j in range(8):
             rows = pl.ds(8 * j, 8)
             wall = pltpu.roll(tiles[j], LANES - q, 1) if q else tiles[j]
-            RW[c, x + 1, rows, :] = RHS[c, x + 1, rows, :] + CW[x + 1, rows, :] * wall
+            values.append(CW[x + 1, rows, :] * wall)
+            RW[c, x + 1, rows, :] = RHS[c, x + 1, rows, :] + values[-1]
+        return values
 
     def take_wall_halo(k):
         both("z", lambda side: wall_z_copy(k, side).wait_send())
@@ -292,14 +325,22 @@
 
     send_wall(0)
 
+    loads[3].wait()
+    take([(src_ref, c, SRC, c) for c in range(3)])
+    both("x", lambda side: src_copy(side).start())
+    loads[4].wait()
+    for a in range(6):
+        IS[0, pl.ds(6 * a, 6), :] = inv_ref[a, :, pl.ds(0, LANES)]
+        IS[1, pl.ds(6 * a, 6), :] = inv_ref[a, :, pl.ds(LANES * (NB - 1), LANES)]
+    both("z", lambda side: inv_copy(side).start())
+    loads[5].wait()
+
     both("x", lambda side: nu_copy(side).wait_send())
     both("x", lambda side: nu_copy(1 - side).wait_recv())
     both("z", lambda side: nz_copy(side).wait_send())
     both("z", lambda side: nz_copy(1 - side).wait_recv())
     corners(lambda a, b: nc_copy(a, b).wait_send())
     corners(lambda a, b: nc_copy(1 - a, 1 - b).wait_recv())
-    both("x", lambda side: src_copy(side).wait_send())
-    both("x", lambda side: src_copy(1 - side).wait_recv())
     y_first = lane % NY == 0
     y_last = lane % NY == NY - 1
     nu_rows = outer(NZR[0], NZR[1])
@@ -358,6 +399,8 @@
         EC[7 + c] = edge_rows(RHS, c, c)
     both("z", lambda side: edge_copy(side).start())
 
+    both("x", lambda side: src_copy(side).wait_send())
+    both("x", lambda side: src_copy(1 - side).wait_recv())
     one_row = lax.broadcasted_iota(jnp.int32, (1, LANES), 1) < LANES // 2
     for side, x in ((0, -1), (1, CX)):
         row = outer(NCR[side, 0, pl.ds(0, 8), :], NCR[side, 1, pl.ds(0, 8), :])[0:1]
@@ -372,19 +415,19 @@
     both("z", lambda side: inv_copy(side).wait_send())
     both("z", lambda side: inv_copy(1 - side).wait_recv())
     for a in range(6):
-        for b in range(6):
-            n = 6 * a + b
-            INV[n, pl.ds(0, NB), :] = inv_ref[a, b]
-            INV[n, pl.ds(NB, 8), :] = ends(IR[1, pl.ds(n, 1), :], IR[0, pl.ds(n, 1), :])
-
-    def plane(c, x, get, put, row):
+        for n in range(NB):
+            INV[pl.ds(6 * a, 6), n, :] = inv_ref[a, :, pl.ds(LANES * n, LANES)]
+    for n in range(36):
+        INV[n, pl.ds(NB, 8), :] = ends(IR[1, pl.ds(n, 1), :], IR[0, pl.ds(n, 1), :])
+
+    def plane(c, x, get, put, row, base=RW):
         tiles = [get(x, j) for j in range(8)]
         for j in range(8):
             rows = pl.ds(8 * j, 8)
             t = tiles[j]
             zm = tiles[j - 1] if j else z_first(row, tiles[7])
             zp = tiles[j + 1] if j < 7 else z_last(row, tiles[0])
-            num = RW[c, x + 1, rows, :] + CF[0, x + 1, rows, :] * get(x - 1, j)
+            num = base[c, x + 1, rows, :] + CF[0, x + 1, rows, :] * get(x - 1, j)
             num = num + CF[1, x + 1, rows, :] * get(x + 1, j)
             num = num + CF[2, x + 1, rows, :] * zm + CF[3, x + 1, rows, :] * zp
             ys = CF[4, x + 1, rows, :] * pltpu.roll(t, 1, 1)
@@ -422,11 +465,11 @@
             UA[c, x, rows, :] = value
         return put
 
-    def middle(p, c, xs, rows):
+    def middle(p, c, xs, rows, base=RW):
         near, far, low, high = rows
         for x in xs:
             row = low if x < 0 else high if x >= CX else near[x : x + 1]
-            plane(c, x, even(p, c), put_odd(c), row)
+            plane(c, x, even(p, c), put_odd(c), row, base)
 
     def middle_rows(p, c, rows):
         near, far, low, high = rows
@@ -446,7 +489,7 @@
         both("x", lambda side: u_copy(p, c, side).wait_send())
         corners(lambda a, b: c_copy(p, c, a, b).wait_send())
         both("z", lambda side: z_copy(p, c, side).wait_send())
-        final((0, 1, CX - 1, CX - 2))
+        final((0, CX - 1))
         edge = [
             jnp.where(one_row, UA[c, x, pl.ds(0, 1), :], UA[c, x, pl.ds(NY - 1, 1), :]) for x in (0, CX - 1)]
         CS[1 - p, c, 0, pl.ds(0, 1), :] = edge[0]
@@ -454,8 +497,13 @@
 
         @pl.when(n + 1 < last)
         def _():
+            corners(lambda a, b: c_copy(1 - p, c, a, b).start())
+
+        final((1, CX - 2))
+
+        @pl.when(n + 1 < last)
+        def _():
             both("x", lambda side: u_copy(1 - p, c, side).start())
-            corners(lambda a, b: c_copy(1 - p, c, a, b).start())
 
         middle(p, c, xs, rows)
         final(range(2, CX - 2))
@@ -466,17 +514,19 @@
         def _():
             both("z", lambda side: z_copy(1 - p, c, side).start())
 
+    def early(k):
+        p = lax.rem(k * (SWEEPS // 2), 2)
+
+        def start(c, carry):
+            arrive(p, c)
+            middle(p, c, range(CX), beside(p, c), RHS)
+            return carry
+
+        lax.fori_loop(0, 3, start, 0)
+
     def first_pair(k):
         n = k * (SWEEPS // 2)
         p = lax.rem(n, 2)
-
-        def start(c, carry):
-            arrive(p, c)
-            middle(p, c, range(CX), beside(p, c))
-            return carry
-
-        lax.fori_loop(0, 3, start, 0)
-        take_wall_halo(k)
 
         def rest(c, carry):
             rows = beside(p, c)
@@ -516,8 +566,19 @@
             SH[a] = total
         return carry
 
+    def give(i, carry):
+        for c in range(3):
+            rows = jnp.concatenate(
+                [UA[c, 2 * i + p, pl.ds(m, 8, stride=8), :] for p in range(2) for m in range(8)], axis=0).T
+            for n in range(8):
+                top, low = rows[8 * n : 8 * n + 8], rows[NY + 8 * n : NY + 8 * n + 8]
+                uout_ref[c, 2 * i, pl.ds(8 * n, 8), :] = jnp.where(half, top, pltpu.roll(low, LANES // 2, 1))
+                uout_ref[c, 2 * i + 1, pl.ds(8 * n, 8), :] = jnp.where(half, pltpu.roll(top, LANES // 2, 1), low)
+        return carry
+
     def subiteration(k, carry):
         take_wall(k)
+        take_wall_halo(k)
         first_pair(k)
         lax.fori_loop(k * (SWEEPS // 2) + 1, (k + 1) * (SWEEPS // 2), pair, 0)
         tiles = [jnp.zeros((8, LANES), F32) for j in range(8)]
@@ -530,12 +591,21 @@
             PULL[pl.ds(j, 8, stride=8), :] = jnp.where(half, tiles[j], 0.0)
             PULL[pl.ds(NY + j, 8, stride=8), :] = jnp.where(half, pltpu.roll(tiles[j], LANES // 2, 1), 0.0)
         pulls = N2[...] * (PULL[...] - WT[...])
-        AS[3 + k] = dot(S[...], pulls.T).reshape(ndev, 8, LANES)
+        AS[3 + k] = pick(S[...], pulls.T).reshape(ndev, 8, LANES)
         exchange_start(3 + k)
+
+        @pl.when(k + 1 < SUBITERS)
+        def _():
+            early(k + 1)
+
+        @pl.when(k + 1 == SUBITERS)
+        def _():
+            lax.fori_loop(0, CX // 2, give, 0)
+
         exchange_wait(3 + k)
-        added = dot(GT[...], AR[3 + k].reshape(8 * ndev, LANES))
+        added = pick(GT[...], AR[3 + k].reshape(8 * ndev, LANES))
         for f in range(6):
-            force = load_ref[f]
+            force = LOAD[f]
             if f < 3:
                 force = force + added[NB * f : NB * (f + 1)]
             FORCE[f, pl.ds(0, NB), :] = force
@@ -557,46 +627,37 @@
         return carry
 
     take_edges()
+    for n in range(NB):
+        LOAD[:, n, :] = load_ref[:, pl.ds(LANES * n, LANES)]
+    early(0)
     lax.fori_loop(0, SUBITERS, subiteration, 0)
 
-    for f in range(6):
-        sout_ref[f] = SH[f, pl.ds(0, NB), :]
-
-    def give(i, carry):
-        for c in range(3):
-            rows = jnp.concatenate(
-                [UA[c, 2 * i + p, pl.ds(m, 8, stride=8), :] for p in range(2) for m in range(8)], axis=0).T
-            for n in range(8):
-                top, low = rows[8 * n : 8 * n + 8], rows[NY + 8 * n : NY + 8 * n + 8]
-                uout_ref[c, 2 * i, pl.ds(8 * n, 8), :] = jnp.where(half, top, pltpu.roll(low, LANES // 2, 1))
-                uout_ref[c, 2 * i + 1, pl.ds(8 * n, 8), :] = jnp.where(half, pltpu.roll(top, LANES // 2, 1), low)
-        return carry
-
-    lax.fori_loop(0, CX // 2, give, 0)
+    for n in range(NB):
+        sout_ref[:, pl.ds(LANES * n, LANES)] = SH[:, n, :]
+
 
 def body(velocity, source, viscosity, owners, targets, shell_load, shell_state, shell_inverse):
     nsec = lax.axis_size("sec")
     ndev = lax.axis_size("dev")
-    owner = owners.reshape(CX)
-    place = jnp.arange(CX, dtype=jnp.int32)
-    earlier = (owner[:, None] == owner[None, :]) & (place[:, None] < place[None, :])
-    rank = jnp.sum(jnp.where(earlier, 1, 0), axis=0).astype(jnp.int32)
-    key = owner * 8 + rank
-    keys = jnp.concatenate([key, key + 2, key + 4, jnp.full((LANES - ROWS,), -1, jnp.int32)])[None, :]
-    name = targets.reshape(CX)
-    names = jnp.concatenate([name, name + NB, name + 2 * NB, jnp.full((LANES - ROWS,), -1, jnp.int32)])[None, :]
-
     vmem = pl.BlockSpec(memory_space=pltpu.VMEM)
+    hbm = pl.BlockSpec(memory_space=pltpu.HBM)
+    bf16 = jnp.bfloat16
     dma = pltpu.SemaphoreType.DMA
     out = pl.pallas_call(
         lambda *refs: kernel(nsec, ndev, *refs),
         out_shape=(
             jax.ShapeDtypeStruct((3, CX, NY, LANES), F32),
-            jax.ShapeDtypeStruct((6, NB, LANES), F32),
+            jax.ShapeDtypeStruct((6, NB * LANES), F32),
         ),
-        in_specs=[vmem] * 8,
+        in_specs=[hbm, hbm, hbm, vmem, vmem, hbm, hbm, hbm],
         out_specs=(vmem, vmem),
         scratch_shapes=[
+            pltpu.VMEM((3, CX, NY, LANES), F32),
+            pltpu.VMEM((3, CX, NY, LANES), F32),
+            pltpu.VMEM((1, CX, NY, LANES), F32),
+            pltpu.VMEM((6, NB * LANES), F32),
+            pltpu.VMEM((6, NB * LANES), F32),
+            pltpu.VMEM((6, 6, NB * LANES), F32),
             pltpu.VMEM((3, CX, NY, LANES), F32),
             pltpu.VMEM((3, CX + 2, NY, LANES), F32),
             pltpu.VMEM((1, CX, NY, LANES), F32),
@@ -620,10 +681,10 @@
             pltpu.VMEM((2, 10, CX, LANES), F32),
             pltpu.VMEM((10, CX, LANES), F32),
             pltpu.VMEM((3, CX, LANES), F32),
-            pltpu.VMEM((8 * ndev, LANES), F32),
-            pltpu.VMEM((LANES, 8 * ndev), F32),
-            pltpu.VMEM((8 * ndev, LANES), F32),
-            pltpu.VMEM((LANES, 8 * ndev), F32),
+            pltpu.VMEM((8 * ndev, LANES), bf16),
+            pltpu.VMEM((LANES, 8 * ndev), bf16),
+            pltpu.VMEM((8 * ndev, LANES), bf16),
+            pltpu.VMEM((LANES, 8 * ndev), bf16),
             pltpu.VMEM((5, ndev, 8, LANES), F32),
             pltpu.VMEM((5, ndev, 8, LANES), F32),
             pltpu.VMEM((LANES, LANES), F32),
@@ -634,6 +695,7 @@
             pltpu.VMEM((LANES, LANES), F32),
             pltpu.VMEM((LANES, LANES), F32),
             pltpu.VMEM((6, 24, LANES), F32),
+            pltpu.VMEM((6, NB, LANES), F32),
             pltpu.VMEM((6, 24, LANES), F32),
             pltpu.VMEM((36, 24, LANES), F32),
             pltpu.VMEM((2, 40, LANES), F32),
@@ -646,16 +708,15 @@
             dma((2,)), dma((2,)), dma((2,)), dma((2,)),
             dma((2, 2)), dma((2, 2)), dma((2, 2)), dma((2, 2)),
             dma((5,)), dma((5,)),
-            dma((2,)), dma((2,)), dma((2, 2)), dma((2, 2)),
+            dma((2,)), dma((2,)), dma((2, 2)), dma((2, 2)), dma((6,)),
         ],
         compiler_params=pltpu.CompilerParams(
             collective_id=0, has_side_effects=True, vmem_limit_bytes=40 * 1024 * 1024),
     )(
-        velocity, source, viscosity[None], keys, names,
-        shell_load.reshape(6, NB, LANES), shell_state.reshape(6, NB, LANES),
-        shell_inverse.reshape(6, 6, NB, LANES),
+        velocity, source, viscosity[None], owners.reshape(1, CX), targets,
+        shell_load, shell_state, shell_inverse,
     )
-    return out[0], out[1].reshape(6, NB * LANES)
+    return tuple(out)
 
 
 def solution(mesh):

time: 109 us -> 103 us (0.945); the launches traced: 109 us -> 101 us
  Pallas kernels: 97.8 us -> 91.1 us
  other arithmetic: 2.87 us -> 0 us
  local copies, waits for them, and re-layouts: 7.63 us -> 9.61 us
    pallas_call x1, Pallas kernels: 97.8 us -> 91.1 us  [body(): pl.pallas_call(lambda *refs: kernel(nsec, ndev, *refs), out_shape=(jax.Sh...]
    unnamed x8 -> x18, local copies, waits for them, and re-layouts: 5.64 us -> 9.61 us
    reshape x2 -> x0, local copies, waits for them, and re-layouts: 1.99 us -> none  [the longest x1 1.09 us: body(): shell_inverse.reshape(6, 6, NB, LANES)]
    add x2 -> x0, other arithmetic: 1.32 us -> none  [the longest x1 0.66 us: body(): key + 2]
where the time goes in v5:
time: 103 us; the launch traced here: 101 us
  Pallas kernels  91.1 us (88%)
  local copies, waits for them, and re-layouts  9.61 us (9%)
    pallas_call x1, Pallas kernels, body(): pl.pallas_call(lambda *refs: kernel(nsec, ndev, *refs), out_shape=(jax.Sh...  91.1 us
    unnamed x18, local copies, waits for them, and re-layouts  9.61 us

profile of v5, /device:TPU:8, one launch (start us, length us, event | category | flops | bytes accessed | tf_op | source)
XLA Modules:
  0.0 101.3 jit_solution(2063622540057120676)
XLA Ops:
  0.6 0.0 copy-start
  0.6 1.4 %copy-done = f32[3,16,64,128]{3,2,1,0:T(8,128)S(1)} copy-done((f32[3,16,64,128]{3,2,1,0:T(8,128)S(1)}, f32[3,16,64,128]{3,2,1,0:T(8,128)}, u32[]{:S(2)}) %copy-start) | copy-done | bytes 1572888
  2.0 0.0 copy-start.1
  2.0 1.4 %copy-done.1 = f32[3,16,64,128]{3,2,1,0:T(8,128)S(1)} copy-done((f32[3,16,64,128]{3,2,1,0:T(8,128)S(1)}, f32[3,16,64,128]{3,2,1,0:T(8,128)}, u32[]{:S(2)}) %copy-start.1) | copy-done | bytes 1572888
  3.5 0.0 copy-start.2
  3.5 1.0 %copy-done.2 = f32[16,64,128]{2,1,0:T(8,128)S(1)} copy-done((f32[16,64,128]{2,1,0:T(8,128)S(1)}, f32[16,64,128]{2,1,0:T(8,128)}, u32[]{:S(2)}) %copy-start.2) | copy-done | bytes 524312
  4.5 0.0 copy-start.3
  4.5 1.0 copy-done.3
  5.5 0.0 copy-start.4
  5.5 0.8 copy-done.4
  6.3 0.0 copy-start.5
  6.3 0.8 copy-done.5
  7.2 0.0 copy-start.6
  7.2 0.7 copy-done.6
  7.8 0.0 copy-start.7
  7.8 0.7 copy-done.7
  8.5 91.1 %shard_map.95 = (f32[3,16,64,128]{3,2,1,0:T(8,128)S(1)}, f32[6,2048]{1,0:T(8,128)S(1)}) custom-call(f32[3,16,64,128]{3,2,1,0:T(8,128)S(1)} %copy-done, f32[3,16,64,128]{3,2,1,0:T(8,128)S(1)} %copy-done.1, f32[1,16,64,128]{3,2,1,0:T(8,128)S(1)} %bitcast.2, s32[1,16]{1,0:T(1,128)S(1)} %bitcast.3, s32[1,16]{1,0:T(1,128)S(1)} %copy-done.7, ...), custom_call_target="tpu_custom_call" | custom-call | tf_op jit(solution)/shard_map/pallas_call | solution.py:646
  99.6 1.1 %copy.12 = f32[3,16,64,128]{3,2,1,0:T(8,128)} copy(f32[3,16,64,128]{3,2,1,0:T(8,128)S(1)} %get-tuple-element.4) | data formatting | bytes 3145728
  100.7 0.6 copy.13
Async XLA Ops:
  0.6 1.4 %copy-start = (f32[3,16,64,128]{3,2,1,0:T(8,128)S(1)}, f32[3,16,64,128]{3,2,1,0:T(8,128)}, u32[]{:S(2)}) copy-start(f32[3,16,64,128]{3,2,1,0:T(8,128)} %refs_0_.1) | copy-start | bytes 4718596
  2.0 1.4 %copy-start.1 = (f32[3,16,64,128]{3,2,1,0:T(8,128)S(1)}, f32[3,16,64,128]{3,2,1,0:T(8,128)}, u32[]{:S(2)}) copy-start(f32[3,16,64,128]{3,2,1,0:T(8,128)} %refs_1_.1) | copy-start | bytes 4718596
  3.5 1.0 %copy-start.2 = (f32[16,64,128]{2,1,0:T(8,128)S(1)}, f32[16,64,128]{2,1,0:T(8,128)}, u32[]{:S(2)}) copy-start(f32[16,64,128]{2,1,0:T(8,128)} %param.10) | copy-start | bytes 1572868
  4.5 1.0 copy-start.3
  5.5 0.8 copy-start.4
  6.3 0.8 copy-start.5
  7.2 0.7 copy-start.6
  7.8 0.7 copy-start.7

commit v6 on v5

--- a/solution.py
+++ b/solution.py
@@ -20,7 +20,7 @@
 def kernel(
     nsec, ndev,
     vel_hbm, src_hbm, nu_hbm, owner_ref, name_ref, load_hbm, state_hbm, inv_hbm,
-    uout_ref, sout_ref,
+    uout_hbm, sout_ref,
     vel_ref, src_ref, nu_ref, load_ref, state_ref, inv_ref,
     UA, UB, NU, CF, CW, SRC, RHS, RW, XR, ZS, ZR, CS, CR,
     NXR, NZS, NZR, NCS, NCR, SXR, EC, ECR, HC, RH,
@@ -566,14 +566,16 @@
             SH[a] = total
         return carry
 
+    store = pltpu.make_async_copy(vel_ref, uout_hbm, in_sem.at[2])
+
     def give(i, carry):
         for c in range(3):
             rows = jnp.concatenate(
                 [UA[c, 2 * i + p, pl.ds(m, 8, stride=8), :] for p in range(2) for m in range(8)], axis=0).T
             for n in range(8):
                 top, low = rows[8 * n : 8 * n + 8], rows[NY + 8 * n : NY + 8 * n + 8]
-                uout_ref[c, 2 * i, pl.ds(8 * n, 8), :] = jnp.where(half, top, pltpu.roll(low, LANES // 2, 1))
-                uout_ref[c, 2 * i + 1, pl.ds(8 * n, 8), :] = jnp.where(half, pltpu.roll(top, LANES // 2, 1), low)
+                vel_ref[c, 2 * i, pl.ds(8 * n, 8), :] = jnp.where(half, top, pltpu.roll(low, LANES // 2, 1))
+                vel_ref[c, 2 * i + 1, pl.ds(8 * n, 8), :] = jnp.where(half, pltpu.roll(top, LANES // 2, 1), low)
         return carry
 
     def subiteration(k, carry):
@@ -601,6 +603,7 @@
         @pl.when(k + 1 == SUBITERS)
         def _():
             lax.fori_loop(0, CX // 2, give, 0)
+            store.start()
 
         exchange_wait(3 + k)
         added = pick(GT[...], AR[3 + k].reshape(8 * ndev, LANES))
@@ -634,6 +637,7 @@
 
     for n in range(NB):
         sout_ref[:, pl.ds(LANES * n, LANES)] = SH[:, n, :]
+    store.wait()
 
 
 def body(velocity, source, viscosity, owners, targets, shell_load, shell_state, shell_inverse):
@@ -650,7 +654,7 @@
             jax.ShapeDtypeStruct((6, NB * LANES), F32),
         ),
         in_specs=[hbm, hbm, hbm, vmem, vmem, hbm, hbm, hbm],
-        out_specs=(vmem, vmem),
+        out_specs=(hbm, vmem),
         scratch_shapes=[
             pltpu.VMEM((3, CX, NY, LANES), F32),
             pltpu.VMEM((3, CX, NY, LANES), F32),
@@ -711,7 +715,7 @@
             dma((2,)), dma((2,)), dma((2, 2)), dma((2, 2)), dma((6,)),
         ],
         compiler_params=pltpu.CompilerParams(
-            collective_id=0, has_side_effects=True, vmem_limit_bytes=40 * 1024 * 1024),
+            collective_id=0, has_side_effects=True, vmem_limit_bytes=60 * 1024 * 1024),
     )(
         velocity, source, viscosity[None], owners.reshape(1, CX), targets,
         shell_load, shell_state, shell_inverse,

time: 103 us -> 96.9 us (0.941)
  local copies, waits for them, and re-layouts: 9.61 us -> 3.39 us
    unnamed x18 -> x4, local copies, waits for them, and re-layouts: 9.61 us -> 3.39 us
where the time goes in v6:
time: 96.9 us; the launch traced here: 95.9 us
  Pallas kernels  91.9 us (95%)
  local copies, waits for them, and re-layouts  3.39 us (3%)
    pallas_call x1, Pallas kernels, body(): pl.pallas_call(lambda *refs: kernel(nsec, ndev, *refs), out_shape=(jax.Sh...  91.9 us
    unnamed x4, local copies, waits for them, and re-layouts  3.39 us

profile of v6, /device:TPU:8, one launch (start us, length us, event | category | flops | bytes accessed | tf_op | source)
XLA Modules:
  0.0 95.9 jit_solution(1215297968398652300)
XLA Ops:
  0.6 91.9 %shard_map.95 = (f32[3,16,64,128]{3,2,1,0:T(8,128)}, f32[6,2048]{1,0:T(8,128)}) custom-call(f32[3,16,64,128]{3,2,1,0:T(8,128)} %refs_0_.1, f32[3,16,64,128]{3,2,1,0:T(8,128)} %refs_1_.1, f32[1,16,64,128]{3,2,1,0:T(8,128)} %bitcast.2, s32[1,16]{1,0:T(1,128)} %bitcast.3, s32[1,16]{1,0:T(1,128)} %refs_4_.1, f32[6,2048]{1,0:T(8,128)} %refs_5_.1, ...), custom_call_target="tpu_custom_call" | custom-call | tf_op jit(solution)/shard_map/pallas_call | solution.py:650
  92.5 0.0 copy-start
  92.5 2.8 %copy.12 = f32[3,16,64,128]{3,2,1,0:T(8,128)} copy(f32[3,16,64,128]{3,2,1,0:T(8,128)} %get-tuple-element.4) | data formatting | bytes 3145728
  95.3 0.0 copy-done
  95.3 0.6 copy.13
Async XLA Ops:
  92.5 2.8 %copy-start = (f32[6,2048]{1,0:T(8,128)S(1)}, f32[6,2048]{1,0:T(8,128)}, u32[]{:S(2)}) copy-start(f32[6,2048]{1,0:T(8,128)} %get-tuple-element.5) | copy-start | bytes 147460

commit v7 on v6

--- a/solution.py
+++ b/solution.py
@@ -39,7 +39,7 @@
 
     def target(axis, side):
         step = 1 if side else -1
-        return {"sec": sec + step} if axis == "x" else {"dev": dev + step}
+        return {"sec": lax.rem(sec + step + nsec, nsec)} if axis == "x" else {"dev": lax.rem(dev + step + ndev, ndev)}
 
     def remote(src, dst, send_sem, recv_sem, device):
         return pltpu.make_async_remote_copy(
@@ -55,7 +55,7 @@
                       zs_sem.at[p, c, side], zr_sem.at[p, c, 1 - side], target("z", side))
 
     def corner(a, b):
-        return {"sec": sec + 2 * a - 1, "dev": dev + 2 * b - 1}
+        return target("x", a) | target("z", b)
 
     def c_copy(p, c, a, b):
         return remote(CS.at[p, c, a], CR.at[p, c, 1 - a, 1 - b],
@@ -104,6 +104,15 @@
             @pl.when(has[(axis, side)])
             def _():
                 act(side)
+
+    def sides(act):
+        for side in (0, 1):
+            act(side)
+
+    def all_corners(act):
+        for a in (0, 1):
+            for b in (0, 1):
+                act(a, b)
 
     def corners(act):
         for a in (0, 1):
@@ -193,8 +202,8 @@
         return carry
 
     lax.fori_loop(1, ndev, greet, 0)
-    both("x", lambda side: pl.semaphore_signal(barrier, inc=1, device_id=target("x", side), device_id_type=MESH))
-    corners(lambda a, b: pl.semaphore_signal(barrier, inc=1, device_id=corner(a, b), device_id_type=MESH))
+    sides(lambda side: pl.semaphore_signal(barrier, inc=1, device_id=target("x", side), device_id_type=MESH))
+    all_corners(lambda a, b: pl.semaphore_signal(barrier, inc=1, device_id=corner(a, b), device_id_type=MESH))
 
     place16 = lax.broadcasted_iota(jnp.int32, (CX, CX), 0)
     other16 = lax.broadcasted_iota(jnp.int32, (CX, CX), 1)
@@ -221,10 +230,6 @@
         S[...], names.astype(jnp.bfloat16), (((1,), (0,)), ((), ())), preferred_element_type=F32
     ).reshape(ndev, 8, LANES)
 
-    sides_x = jnp.where(has[("x", 0)], 1, 0) + jnp.where(has[("x", 1)], 1, 0)
-    sides_z = jnp.where(has[("z", 0)], 1, 0) + jnp.where(has[("z", 1)], 1, 0)
-    pl.semaphore_wait(barrier, (ndev - 1) + sides_x + sides_x * sides_z)
-    exchange_start(0)
 
     def take(refs):
         def step(i, carry):
@@ -246,6 +251,9 @@
     take([(nu_ref, 0, NU, 0)])
     NZS[...] = face_rows(NU, 0, 0, NY - 1)
     send_corner(NCS, NZS[...])
+
+    pl.semaphore_wait(barrier, (ndev - 1) + 6)
+    exchange_start(0)
     corners(lambda a, b: nc_copy(a, b).start())
     both("z", lambda side: nz_copy(side).start())
     both("x", lambda side: nu_copy(side).start())
@@ -258,9 +266,9 @@
         ZS[0, c, pl.ds(0, CX), :] = face_rows(UA, c, 0, NY - 1)
         ZS[0, c, pl.ds(CX, CX), :] = face_rows(UA, c, 8, NY - 9)
         send_corner(CS.at[0, c], ZS[0, c, pl.ds(0, CX), :])
-        corners(lambda a, b: c_copy(0, c, a, b).start())
-        both("z", lambda side: z_copy(0, c, side).start())
-        both("x", lambda side: u_copy(0, c, side).start())
+        all_corners(lambda a, b: c_copy(0, c, a, b).start())
+        sides(lambda side: z_copy(0, c, side).start())
+        sides(lambda side: u_copy(0, c, side).start())
 
     loads[0].wait()
     SH[...] = jnp.zeros(SH.shape, F32)
@@ -281,7 +289,7 @@
         AS[1 + k] = pick(G[...], tall(rows)).reshape(ndev, 8, LANES)
         exchange_start(1 + k)
 
-    def take_wall(k):
+    def take_wall(k, begun):
         exchange_wait(1 + k)
         wall = pick(ST[...], AR[1 + k].reshape(8 * ndev, LANES))
         WQ[k] = wall[:ROWS]
@@ -298,7 +306,8 @@
             for x in range(CX):
                 for j, value in enumerate(add_wall(c, x, c * CX + x, tiles)):
                     rows = pl.ds(8 * j, 8)
-                    UB[c, x + 1, rows, :] = UB[c, x + 1, rows, :] + value
+                    if begun:
+                        UB[c, x + 1, rows, :] = UB[c, x + 1, rows, :] + value
 
     def add_wall(c, x, q, tiles):
         values = []
@@ -344,6 +353,10 @@
     y_first = lane % NY == 0
     y_last = lane % NY == NY - 1
     nu_rows = outer(NZR[0], NZR[1])
+    z_low = jnp.where((sub == 0) & half, jnp.where(has[("z", 0)], 1.0, 0.0), 1.0)
+    z_high = jnp.where((sub == 7) & ~half, jnp.where(has[("z", 1)], 1.0, 0.0), 1.0)
+    x_low = jnp.where(has[("x", 0)], 1.0, 0.0)
+    x_high = jnp.where(has[("x", 1)], 1.0, 0.0)
 
     def halo_planes(ref, c, near):
         def get(x, j):
@@ -371,8 +384,11 @@
             for f in faces[1:]:
                 total = total + f
             inverse = valid / total
+            ends_at = [x_low if x == 0 else None, x_high if x == CX - 1 else None,
+                       z_low if j == 0 else None, z_high if j == 7 else None]
             for n in range(4):
-                CF[n, x + 1, rows, :] = faces[n] * inverse
+                face = faces[n] * inverse
+                CF[n, x + 1, rows, :] = face if ends_at[n] is None else face * ends_at[n]
             below = faces[4] * inverse
             CW[x + 1, rows, :] = jnp.where(y_first, below, 0.0)
             CF[4, x + 1, rows, :] = jnp.where(y_first, 0.0, below)
@@ -411,14 +427,6 @@
         both("z", lambda side: edge_copy(1 - side).wait_recv())
         for i in range(10):
             HC[i] = outer(ECR[0, i], ECR[1, i])
-
-    both("z", lambda side: inv_copy(side).wait_send())
-    both("z", lambda side: inv_copy(1 - side).wait_recv())
-    for a in range(6):
-        for n in range(NB):
-            INV[pl.ds(6 * a, 6), n, :] = inv_ref[a, :, pl.ds(LANES * n, LANES)]
-    for n in range(36):
-        INV[n, pl.ds(NB, 8), :] = ends(IR[1, pl.ds(n, 1), :], IR[0, pl.ds(n, 1), :])
 
     def plane(c, x, get, put, row, base=RW):
         tiles = [get(x, j) for j in range(8)]
@@ -438,16 +446,19 @@
     last = SUBITERS * SWEEPS // 2
 
     def arrive(p, c):
-        both("z", lambda side: z_copy(p, c, 1 - side).wait_recv())
-        both("x", lambda side: u_copy(p, c, 1 - side).wait_recv())
-        corners(lambda a, b: c_copy(p, c, 1 - a, 1 - b).wait_recv())
+        sides(lambda side: z_copy(p, c, 1 - side).wait_recv())
+        sides(lambda side: u_copy(p, c, 1 - side).wait_recv())
 
     def beside(p, c):
         near = outer(ZR[p, c, 0, pl.ds(0, CX), :], ZR[p, c, 1, pl.ds(0, CX), :])
         far = outer(ZR[p, c, 0, pl.ds(CX, CX), :], ZR[p, c, 1, pl.ds(CX, CX), :])
+        return near, far
+
+    def beside_corners(p, c):
+        all_corners(lambda a, b: c_copy(p, c, 1 - a, 1 - b).wait_recv())
         low = outer(CR[p, c, 0, 0], CR[p, c, 0, 1])[0:1]
         high = outer(CR[p, c, 1, 0], CR[p, c, 1, 1])[0:1]
-        return near, far, low, high
+        return low, high
 
     def even(p, c):
         return halo_planes(UA, c, lambda side, n, rows: XR[p, c, side, n, rows, :])
@@ -466,29 +477,29 @@
         return put
 
     def middle(p, c, xs, rows, base=RW):
-        near, far, low, high = rows
         for x in xs:
-            row = low if x < 0 else high if x >= CX else near[x : x + 1]
+            row = rows[0] if x < 0 else rows[1] if x >= CX else rows[0][x : x + 1]
             plane(c, x, even(p, c), put_odd(c), row, base)
 
-    def middle_rows(p, c, rows):
-        near, far, low, high = rows
+    def middle_rows(p, c, rows, ends_of):
+        near, far = rows
+        low, high = ends_of
         before = jnp.where(sub16 == 0, low, pltpu.roll(near, 1, 0))
         after = jnp.where(sub16 == CX - 1, high, pltpu.roll(near, CX - 1, 0))
         total = RH[c] + HC[0] * before + HC[1] * after + HC[2] * far
         total = total + HC[3] * ZS[p, c, pl.ds(0, CX), :]
         return total + HC[4] * pltpu.roll(near, 1, 1) + HC[5] * pltpu.roll(near, LANES - 1, 1)
 
-    def finish(n, p, c, rows, xs):
-        near = middle_rows(p, c, rows)
+    def finish(n, p, c, rows, ends_of, xs):
+        near = middle_rows(p, c, rows, ends_of)
 
         def final(group):
             for x in group:
                 plane(c, x, odd(c), put_even(c), near[x : x + 1])
 
-        both("x", lambda side: u_copy(p, c, side).wait_send())
-        corners(lambda a, b: c_copy(p, c, a, b).wait_send())
-        both("z", lambda side: z_copy(p, c, side).wait_send())
+        sides(lambda side: u_copy(p, c, side).wait_send())
+        all_corners(lambda a, b: c_copy(p, c, a, b).wait_send())
+        sides(lambda side: z_copy(p, c, side).wait_send())
         final((0, CX - 1))
         edge = [
             jnp.where(one_row, UA[c, x, pl.ds(0, 1), :], UA[c, x, pl.ds(NY - 1, 1), :]) for x in (0, CX - 1)]
@@ -497,13 +508,13 @@
 
         @pl.when(n + 1 < last)
         def _():
-            corners(lambda a, b: c_copy(1 - p, c, a, b).start())
+            all_corners(lambda a, b: c_copy(1 - p, c, a, b).start())
 
         final((1, CX - 2))
 
         @pl.when(n + 1 < last)
         def _():
-            both("x", lambda side: u_copy(1 - p, c, side).start())
+            sides(lambda side: u_copy(1 - p, c, side).start())
 
         middle(p, c, xs, rows)
         final(range(2, CX - 2))
@@ -512,14 +523,14 @@
 
         @pl.when(n + 1 < last)
         def _():
-            both("z", lambda side: z_copy(1 - p, c, side).start())
-
-    def early(k):
+            sides(lambda side: z_copy(1 - p, c, side).start())
+
+    def early(k, base):
         p = lax.rem(k * (SWEEPS // 2), 2)
 
         def start(c, carry):
             arrive(p, c)
-            middle(p, c, range(CX), beside(p, c), RHS)
+            middle(p, c, range(CX), beside(p, c), base)
             return carry
 
         lax.fori_loop(0, 3, start, 0)
@@ -529,9 +540,9 @@
         p = lax.rem(n, 2)
 
         def rest(c, carry):
-            rows = beside(p, c)
-            middle(p, c, (-1, CX), rows)
-            finish(n, p, c, rows, ())
+            ends_of = beside_corners(p, c)
+            middle(p, c, (-1, CX), ends_of)
+            finish(n, p, c, beside(p, c), ends_of, ())
             return carry
 
         lax.fori_loop(0, 3, rest, 0)
@@ -542,8 +553,10 @@
         def component(c, carry):
             arrive(p, c)
             rows = beside(p, c)
-            middle(p, c, (-1, 0, 1, 2, CX, CX - 1, CX - 2, CX - 3), rows)
-            finish(n, p, c, rows, range(3, CX - 3))
+            middle(p, c, (0, 1, 2, CX - 1, CX - 2, CX - 3), rows)
+            ends_of = beside_corners(p, c)
+            middle(p, c, (-1, CX), ends_of)
+            finish(n, p, c, rows, ends_of, range(3, CX - 3))
             return carry
 
         lax.fori_loop(0, 3, component, 0)
@@ -578,8 +591,22 @@
                 vel_ref[c, 2 * i + 1, pl.ds(8 * n, 8), :] = jnp.where(half, pltpu.roll(top, LANES // 2, 1), low)
         return carry
 
+    def build_shell():
+        both("z", lambda side: inv_copy(side).wait_send())
+        both("z", lambda side: inv_copy(1 - side).wait_recv())
+        for a in range(6):
+            for n in range(NB):
+                INV[pl.ds(6 * a, 6), n, :] = inv_ref[a, :, pl.ds(LANES * n, LANES)]
+        for n in range(36):
+            INV[n, pl.ds(NB, 8), :] = ends(IR[1, pl.ds(n, 1), :], IR[0, pl.ds(n, 1), :])
+        for n in range(NB):
+            LOAD[:, n, :] = load_ref[:, pl.ds(LANES * n, LANES)]
+
     def subiteration(k, carry):
-        take_wall(k)
+        @pl.when(k > 0)
+        def _():
+            take_wall(k, True)
+
         take_wall_halo(k)
         first_pair(k)
         lax.fori_loop(k * (SWEEPS // 2) + 1, (k + 1) * (SWEEPS // 2), pair, 0)
@@ -598,7 +625,8 @@
 
         @pl.when(k + 1 < SUBITERS)
         def _():
-            early(k + 1)
+            early(k + 1, RHS)
+            build_shell()
 
         @pl.when(k + 1 == SUBITERS)
         def _():
@@ -629,10 +657,9 @@
             send_wall(k + 1)
         return carry
 
+    take_wall(0, False)
+    early(0, RW)
     take_edges()
-    for n in range(NB):
-        LOAD[:, n, :] = load_ref[:, pl.ds(LANES * n, LANES)]
-    early(0)
     lax.fori_loop(0, SUBITERS, subiteration, 0)
 
     for n in range(NB):

time: 96.9 us -> 97.2 us (level)
  no operation moved by 1% of the time
where the time goes in v7:
time: 97.2 us; the launch traced here: 95.8 us
  Pallas kernels  91.8 us (94%)
  local copies, waits for them, and re-layouts  3.39 us (3%)
    pallas_call x1, Pallas kernels, body(): pl.pallas_call(lambda *refs: kernel(nsec, ndev, *refs), out_shape=(jax.Sh...  91.8 us
    unnamed x4, local copies, waits for them, and re-layouts  3.39 us

profile of v7, /device:TPU:8, one launch (start us, length us, event | category | flops | bytes accessed | tf_op | source)
XLA Modules:
  0.0 95.8 jit_solution(15202556395242742802)
XLA Ops:
  0.6 91.8 %shard_map.95 = (f32[3,16,64,128]{3,2,1,0:T(8,128)}, f32[6,2048]{1,0:T(8,128)}) custom-call(f32[3,16,64,128]{3,2,1,0:T(8,128)} %refs_0_.1, f32[3,16,64,128]{3,2,1,0:T(8,128)} %refs_1_.1, f32[1,16,64,128]{3,2,1,0:T(8,128)} %bitcast.2, s32[1,16]{1,0:T(1,128)} %bitcast.3, s32[1,16]{1,0:T(1,128)} %refs_4_.1, f32[6,2048]{1,0:T(8,128)} %refs_5_.1, ...), custom_call_target="tpu_custom_call" | custom-call | tf_op jit(solution)/shard_map/pallas_call | solution.py:677
  92.4 0.0 copy-start
  92.5 2.8 %copy.12 = f32[3,16,64,128]{3,2,1,0:T(8,128)} copy(f32[3,16,64,128]{3,2,1,0:T(8,128)} %get-tuple-element.4) | data formatting | bytes 3145728
  95.2 0.0 copy-done
  95.2 0.6 copy.13
Async XLA Ops:
  92.4 2.8 %copy-start = (f32[6,2048]{1,0:T(8,128)S(1)}, f32[6,2048]{1,0:T(8,128)}, u32[]{:S(2)}) copy-start(f32[6,2048]{1,0:T(8,128)} %get-tuple-element.5) | copy-start | bytes 147460

commit v8 on v7

--- a/solution.py
+++ b/solution.py
@@ -122,15 +122,13 @@
                     act(a, b)
 
     def exchange_start(phase):
-        def send(i, carry):
+        def hops(i):
+            y, z = i // 8, i // 2 % 4
+            return min(y, 4 - y) + min(z, 4 - z)
+
+        for i in sorted(range(1, ndev), key=lambda i: -hops(i)):
             peer = lax.rem(dev + i, ndev)
-            pltpu.make_async_remote_copy(
-                src_ref=AS.at[phase, peer], dst_ref=AR.at[phase, dev],
-                send_sem=as_sem.at[phase], recv_sem=ar_sem.at[phase],
-                device_id={"dev": peer}, device_id_type=MESH).start()
-            return carry
-
-        lax.fori_loop(1, ndev, send, 0)
+            remote(AS.at[phase, peer], AR.at[phase, dev], as_sem.at[phase], ar_sem.at[phase], {"dev": peer}).start()
         AR[phase, dev] = AS[phase, dev]
 
     def exchange_wait(phase):
@@ -188,7 +186,7 @@
     for copy in loads:
         copy.start()
 
-    for ref in (XR, ZR, CR, NXR, NZR, NCR, SXR, ECR, WXR, WZR, CS, NCS):
+    for ref in (NXR, NZR, NCR, SXR, ECR, WXR, WZR, CS, NCS):
         ref[...] = jnp.zeros(ref.shape, F32)
     IR[...] = jnp.zeros(IR.shape, F32)
     IS[...] = jnp.zeros(IS.shape, F32)
@@ -282,7 +280,6 @@
     exchange_wait(0)
     got = AR[0].reshape(8 * ndev, LANES)
     G[...] = got.astype(jnp.bfloat16)
-    GT[...] = got.T.astype(jnp.bfloat16)
 
     def send_wall(k):
         rows = jnp.concatenate([SH[f, pl.ds(0, NB), :] for f in range(3)], axis=0)
@@ -333,6 +330,7 @@
                 add_wall(c, x, c * CX + own, tiles)
 
     send_wall(0)
+    GT[...] = got.T.astype(jnp.bfloat16)
 
     loads[3].wait()
     take([(src_ref, c, SRC, c) for c in range(3)])
@@ -428,9 +426,9 @@
         for i in range(10):
             HC[i] = outer(ECR[0, i], ECR[1, i])
 
-    def plane(c, x, get, put, row, base=RW):
+    def plane(c, x, get, put, row, base=RW, js=range(8)):
         tiles = [get(x, j) for j in range(8)]
-        for j in range(8):
+        for j in js:
             rows = pl.ds(8 * j, 8)
             t = tiles[j]
             zm = tiles[j - 1] if j else z_first(row, tiles[7])
@@ -476,10 +474,10 @@
             UA[c, x, rows, :] = value
         return put
 
-    def middle(p, c, xs, rows, base=RW):
+    def middle(p, c, xs, rows, base=RW, js=range(8)):
         for x in xs:
-            row = rows[0] if x < 0 else rows[1] if x >= CX else rows[0][x : x + 1]
-            plane(c, x, even(p, c), put_odd(c), row, base)
+            row = None if rows is None else rows[0] if x < 0 else rows[1] if x >= CX else rows[0][x : x + 1]
+            plane(c, x, even(p, c), put_odd(c), row, base, js)
 
     def middle_rows(p, c, rows, ends_of):
         near, far = rows
@@ -551,12 +549,15 @@
         p = lax.rem(n, 2)
 
         def component(c, carry):
-            arrive(p, c)
+            middle(p, c, range(1, CX - 1), None, js=range(1, 7))
+            sides(lambda side: z_copy(p, c, 1 - side).wait_recv())
             rows = beside(p, c)
-            middle(p, c, (0, 1, 2, CX - 1, CX - 2, CX - 3), rows)
+            middle(p, c, range(1, CX - 1), rows, js=(0, 7))
+            sides(lambda side: u_copy(p, c, 1 - side).wait_recv())
+            middle(p, c, (0, CX - 1), rows)
             ends_of = beside_corners(p, c)
             middle(p, c, (-1, CX), ends_of)
-            finish(n, p, c, rows, ends_of, range(3, CX - 3))
+            finish(n, p, c, rows, ends_of, ())
             return carry
 
         lax.fori_loop(0, 3, component, 0)

time: 97.2 us -> 95.5 us (0.983)
  Pallas kernels: 91.8 us -> 90.3 us
    pallas_call x1, Pallas kernels: 91.8 us -> 90.3 us  [body(): pl.pallas_call(lambda *refs: kernel(nsec, ndev, *refs), out_shape=(jax.Sh...]
where the time goes in v8:
time: 95.5 us; the launch traced here: 94.3 us
  Pallas kernels  90.3 us (95%)
  local copies, waits for them, and re-layouts  3.39 us (4%)
    pallas_call x1, Pallas kernels, body(): pl.pallas_call(lambda *refs: kernel(nsec, ndev, *refs), out_shape=(jax.Sh...  90.3 us
    unnamed x4, local copies, waits for them, and re-layouts  3.39 us

profile of v8, /device:TPU:8, one launch (start us, length us, event | category | flops | bytes accessed | tf_op | source)
XLA Modules:
  0.0 94.3 jit_solution(10274569643413759039)
XLA Ops:
  0.6 90.3 %shard_map.95 = (f32[3,16,64,128]{3,2,1,0:T(8,128)}, f32[6,2048]{1,0:T(8,128)}) custom-call(f32[3,16,64,128]{3,2,1,0:T(8,128)} %refs_0_.1, f32[3,16,64,128]{3,2,1,0:T(8,128)} %refs_1_.1, f32[1,16,64,128]{3,2,1,0:T(8,128)} %bitcast.2, s32[1,16]{1,0:T(1,128)} %bitcast.3, s32[1,16]{1,0:T(1,128)} %refs_4_.1, f32[6,2048]{1,0:T(8,128)} %refs_5_.1, ...), custom_call_target="tpu_custom_call" | custom-call | tf_op jit(solution)/shard_map/pallas_call | solution.py:678
  90.9 0.0 copy-start
  91.0 2.8 %copy.12 = f32[3,16,64,128]{3,2,1,0:T(8,128)} copy(f32[3,16,64,128]{3,2,1,0:T(8,128)} %get-tuple-element.4) | data formatting | bytes 3145728
  93.7 0.0 copy-done
  93.7 0.6 copy.13
Async XLA Ops:
  90.9 2.8 %copy-start = (f32[6,2048]{1,0:T(8,128)S(1)}, f32[6,2048]{1,0:T(8,128)}, u32[]{:S(2)}) copy-start(f32[6,2048]{1,0:T(8,128)} %get-tuple-element.5) | copy-start | bytes 147460

commit v9 on v8

--- a/solution.py
+++ b/solution.py
@@ -491,9 +491,9 @@
     def finish(n, p, c, rows, ends_of, xs):
         near = middle_rows(p, c, rows, ends_of)
 
-        def final(group):
+        def final(group, js=range(8)):
             for x in group:
-                plane(c, x, odd(c), put_even(c), near[x : x + 1])
+                plane(c, x, odd(c), put_even(c), near[x : x + 1], js=js)
 
         sides(lambda side: u_copy(p, c, side).wait_send())
         all_corners(lambda a, b: c_copy(p, c, a, b).wait_send())
@@ -515,13 +515,15 @@
             sides(lambda side: u_copy(1 - p, c, side).start())
 
         middle(p, c, xs, rows)
-        final(range(2, CX - 2))
+        final(range(2, CX - 2), (0, 1, 6, 7))
         ZS[1 - p, c, pl.ds(0, CX), :] = face_rows(UA, c, 0, NY - 1)
         ZS[1 - p, c, pl.ds(CX, CX), :] = face_rows(UA, c, 8, NY - 9)
 
         @pl.when(n + 1 < last)
         def _():
             sides(lambda side: z_copy(1 - p, c, side).start())
+
+        final(range(2, CX - 2), (2, 3, 4, 5))
 
     def early(k, base):
         p = lax.rem(k * (SWEEPS // 2), 2)

time: 95.5 us -> 95.6 us (level)
  no operation moved by 1% of the time
where the time goes in v9:
time: 95.6 us; the launch traced here: 94.6 us
  Pallas kernels  90.5 us (95%)
  local copies, waits for them, and re-layouts  3.39 us (4%)
    pallas_call x1, Pallas kernels, body(): pl.pallas_call(lambda *refs: kernel(nsec, ndev, *refs), out_shape=(jax.Sh...  90.5 us
    unnamed x4, local copies, waits for them, and re-layouts  3.39 us

profile of v9, /device:TPU:8, one launch (start us, length us, event | category | flops | bytes accessed | tf_op | source)
XLA Modules:
  0.0 94.6 jit_solution(5245445961376457797)
XLA Ops:
  0.6 90.5 %shard_map.95 = (f32[3,16,64,128]{3,2,1,0:T(8,128)}, f32[6,2048]{1,0:T(8,128)}) custom-call(f32[3,16,64,128]{3,2,1,0:T(8,128)} %refs_0_.1, f32[3,16,64,128]{3,2,1,0:T(8,128)} %refs_1_.1, f32[1,16,64,128]{3,2,1,0:T(8,128)} %bitcast.2, s32[1,16]{1,0:T(1,128)} %bitcast.3, s32[1,16]{1,0:T(1,128)} %refs_4_.1, f32[6,2048]{1,0:T(8,128)} %refs_5_.1, ...), custom_call_target="tpu_custom_call" | custom-call | tf_op jit(solution)/shard_map/pallas_call | solution.py:680
  91.2 0.0 copy-start
  91.2 2.8 %copy.12 = f32[3,16,64,128]{3,2,1,0:T(8,128)} copy(f32[3,16,64,128]{3,2,1,0:T(8,128)} %get-tuple-element.4) | data formatting | bytes 3145728
  93.9 0.0 copy-done
  93.9 0.6 copy.13
Async XLA Ops:
  91.2 2.8 %copy-start = (f32[6,2048]{1,0:T(8,128)S(1)}, f32[6,2048]{1,0:T(8,128)}, u32[]{:S(2)}) copy-start(f32[6,2048]{1,0:T(8,128)} %get-tuple-element.5) | copy-start | bytes 147460
